TPU v7x, 128 devices: a whole 4x4x4 slice. The times are simulated.
128 devices in a mesh: dp: 8 (over y_hi, x), tensor: 16 (over y_lo, z, core).
Axes of the slice: x: 4, y: 4 (y_hi: 2, y_lo: 2; y = y_hi * 2 + y_lo), z: 4, core: 2. Of those that a mesh axis runs over, the one named last changes fastest.
Arguments:
- images: bfloat16 [16384, 768], P('dp'), may hold values from -6 to 6
- head: bfloat16 [768, 768], P(None, 'tensor'), may hold values from -0.21875 to 0.21875
- tea_img: bfloat16 [16384, 1536], P('dp'), may hold values from -6 to 6
- stu_txt: bfloat16 [16384, 768], P(('dp', 'tensor')), may hold values from -6 to 6
- tea_txt: bfloat16 [16384, 1536], P(('dp', 'tensor')), may hold values from -6 to 6
Outputs:
- grad_images: float32 [16384, 768], P(('dp', 'tensor'))
- grad_head: float32 [768, 768], P(None, 'tensor')
- grad_text: float32 [16384, 768], P(('dp', 'tensor'))
All inputs are finite; a program needn't handle non-finite values.
Results may differ from a plain program's by a relative error of at most 0.012.
Values may be sent and summed in bfloat16 or wider, within the bound.
A program may use at most 192 MiB of HBM per device.

v0:
```python
import jax
import jax.numpy as jnp
from jax import lax
from jax.sharding import PartitionSpec as P

logit_scale = 64.0
logit_bias = -2.0
loss_scale = 65536.0


def passed_along(value, axis, steps):
    count = lax.axis_size(axis)
    pairs = [(source, (source + steps) % count) for source in range(count)]
    return lax.ppermute(value, axis, pairs)


def normalize(values):
    floats = values.astype(jnp.float32)
    length = jnp.sqrt(jnp.sum(floats * floats, axis=1, keepdims=True) + 1e-06)
    return (floats / length, length)


def affinity_tile(img_emb, tea_img_emb, txt_piece, tea_piece, factor):
    contract = (((1,), (1,)), ((), ()))
    target = jax.nn.sigmoid(
        logit_scale
        * lax.dot_general(tea_img_emb, tea_piece, contract, preferred_element_type=jnp.float32)
        + logit_bias
    )
    student = (
        logit_scale
        * lax.dot_general(img_emb, txt_piece, contract, preferred_element_type=jnp.float32)
        + logit_bias
    )
    return ((jax.nn.sigmoid(student) - target) * factor).astype(jnp.bfloat16)


def transpose_product(coef, img_emb):
    return lax.dot_general(
        coef, img_emb, (((0,), (0,)), ((), ())), preferred_element_type=jnp.float32
    )


def per_device(images, head, tea_img, stu_txt, tea_txt):
    dp_count = lax.axis_size("dp")
    tensor_count = lax.axis_size("tensor")
    tensor_rank = lax.axis_index("tensor")
    rows = images.shape[0]
    columns = head.shape[1]
    emb_width = columns * tensor_count
    factor = logit_scale * loss_scale / (rows * dp_count)
    proj_local = jnp.dot(images, head, preferred_element_type=jnp.float32).astype(jnp.bfloat16)
    proj = lax.all_gather(proj_local, "tensor", axis=1, tiled=True)
    img_unit, proj_norm = normalize(proj)
    img_emb = img_unit.astype(jnp.bfloat16)
    tea_img_emb = normalize(tea_img)[0].astype(jnp.bfloat16)
    txt_unit, txt_norm = normalize(stu_txt)
    txt_emb = txt_unit.astype(jnp.bfloat16)
    tea_txt_emb = normalize(tea_txt)[0].astype(jnp.bfloat16)
    img_grads = jnp.zeros((rows, emb_width), jnp.float32)
    text_grads = jnp.zeros((stu_txt.shape[0], emb_width), jnp.float32)
    travel_emb = txt_emb
    travel_tea = tea_txt_emb
    for rotation in range(dp_count):
        coef = affinity_tile(img_emb, tea_img_emb, travel_emb, travel_tea, factor)
        img_grads = img_grads + jnp.dot(coef, travel_emb, preferred_element_type=jnp.float32)
        text_grads = text_grads + transpose_product(coef, img_emb)
        if rotation + 1 < dp_count:
            travel_emb, travel_tea = passed_along((travel_emb, travel_tea), "dp", 1)
            text_grads = passed_along(text_grads, "dp", 1)
        else:
            text_grads = passed_along(text_grads, "dp", 1)
    share = rows // tensor_count
    summed = lax.psum(img_grads, "tensor")
    row_dot = jnp.sum(img_unit * summed, axis=1, keepdims=True)
    grad_proj = ((summed - img_unit * row_dot) / proj_norm).astype(jnp.bfloat16)
    own_columns = lax.dynamic_slice_in_dim(grad_proj, tensor_rank * columns, columns, 1)
    head_part = lax.dot_general(
        images, own_columns, (((0,), (0,)), ((), ())), preferred_element_type=jnp.float32
    )
    own_rows = lax.dynamic_slice_in_dim(grad_proj, tensor_rank * share, share, 0)
    head_full = lax.all_gather(head, "tensor", axis=1, tiled=True)
    grad_images = lax.dot_general(
        own_rows, head_full, (((1,), (1,)), ((), ())), preferred_element_type=jnp.float32
    )
    grad_head = lax.psum(head_part, "dp")
    grad_text = (
        text_grads - txt_unit * jnp.sum(txt_unit * text_grads, axis=1, keepdims=True)
    ) / txt_norm
    return (grad_images, grad_head, grad_text)


def solution(mesh):
    placed = (
        P("dp", None),
        P(None, "tensor"),
        P("dp", None),
        P(("dp", "tensor"), None),
        P(("dp", "tensor"), None),
    )
    return jax.shard_map(
        per_device,
        mesh=mesh,
        in_specs=placed,
        out_specs=(P(("dp", "tensor"), None), P(None, "tensor"), P(("dp", "tensor"), None)),
        check_vma=False,
    )
```

profile of v0, /device:TPU:0, one launch (start us, length us, event | category | flops | bytes accessed | tf_op | source)
XLA Modules:
  0.0 517.0 jit_solution(16663711193488015860)
XLA Ops:
  9.1 2.6 convolution_convert_fusion
  18.0 4.1 fusion
  22.1 11.4 %collective-permute-done = bf16[128,768]{1,0:T(8,128)(2,1)S(1)} collective-permute-done((bf16[128,768]{1,0:T(8,128)(2,1)S(1)}, bf16[128,768]{1,0:T(8,128)(2,1)S(1)}, u32[]{:S(2)}, u32[]{:S(2)}) %collective-permute-start) | collective-permute-done | bytes 196640 | tf_op jit(solution)/shard_map/ppermute | solution.py:14
  33.5 9.6 %collective-permute-done.2 = bf16[128,768]{1,0:T(8,128)(2,1)S(1)} collective-permute-done((bf16[128,768]{1,0:T(8,128)(2,1)S(1)}, bf16[128,768]{1,0:T(8,128)(2,1)S(1)}, u32[]{:S(2)}, u32[]{:S(2)}) %collective-permute-start.2) | collective-permute-done | bytes 196640 | tf_op jit(solution)/shard_map/ppermute | solution.py:14
  43.1 2.9 fusion.1
  46.0 6.5 %collective-permute-done.4 = bf16[128,768]{1,0:T(8,128)(2,1)S(1)} collective-permute-done((bf16[128,768]{1,0:T(8,128)(2,1)S(1)}, bf16[128,768]{1,0:T(8,128)(2,1)S(1)}, u32[]{:S(2)}, u32[]{:S(2)}) %collective-permute-start.4) | collective-permute-done | bytes 196640 | tf_op jit(solution)/shard_map/ppermute | solution.py:14
  52.5 2.8 fusion.98
  55.3 8.7 %collective-permute-done.6 = bf16[128,768]{1,0:T(8,128)(2,1)S(1)} collective-permute-done((bf16[128,768]{1,0:T(8,128)(2,1)S(1)}, bf16[128,768]{1,0:T(8,128)(2,1)S(1)}, u32[]{:S(2)}, u32[]{:S(2)}) %collective-permute-start.6) | collective-permute-done | bytes 196640 | tf_op jit(solution)/shard_map/ppermute | solution.py:14
  64.0 2.9 fusion.96
  66.9 4.4 collective-permute-done.3
  71.3 3.3 collective-permute-done.8
  75.0 2.8 fusion.94
  77.8 6.3 %collective-permute-done.5 = bf16[128,1536]{1,0:T(8,128)(2,1)S(1)} collective-permute-done((bf16[128,1536]{1,0:T(8,128)(2,1)S(1)}, bf16[128,1536]{1,0:T(8,128)(2,1)S(1)}, u32[]{:S(2)}, u32[]{:S(2)}) %collective-permute-start.5) | collective-permute-done | bytes 393248 | tf_op jit(solution)/shard_map/ppermute | solution.py:14
  84.1 4.3 collective-permute-done.10
  88.4 2.8 fusion.92
  91.3 5.5 %collective-permute-done.7 = bf16[128,1536]{1,0:T(8,128)(2,1)S(1)} collective-permute-done((bf16[128,1536]{1,0:T(8,128)(2,1)S(1)}, bf16[128,1536]{1,0:T(8,128)(2,1)S(1)}, u32[]{:S(2)}, u32[]{:S(2)}) %collective-permute-start.7) | collective-permute-done | bytes 393248 | tf_op jit(solution)/shard_map/ppermute | solution.py:14
  96.8 2.8 fusion.90
  99.6 8.7 %collective-permute-done.9 = bf16[128,1536]{1,0:T(8,128)(2,1)S(1)} collective-permute-done((bf16[128,1536]{1,0:T(8,128)(2,1)S(1)}, bf16[128,1536]{1,0:T(8,128)(2,1)S(1)}, u32[]{:S(2)}, u32[]{:S(2)}) %collective-permute-start.9) | collective-permute-done | bytes 393248 | tf_op jit(solution)/shard_map/ppermute | solution.py:14
  108.3 2.9 fusion.88
  111.1 8.8 %collective-permute-done.11 = bf16[128,1536]{1,0:T(8,128)(2,1)S(1)} collective-permute-done((bf16[128,1536]{1,0:T(8,128)(2,1)S(1)}, bf16[128,1536]{1,0:T(8,128)(2,1)S(1)}, u32[]{:S(2)}, u32[]{:S(2)}) %collective-permute-start.11) | collective-permute-done | bytes 393248 | tf_op jit(solution)/shard_map/ppermute | solution.py:14
  120.1 2.8 fusion.86
  122.9 8.6 %collective-permute-done.13 = bf16[128,1536]{1,0:T(8,128)(2,1)S(1)} collective-permute-done((bf16[128,1536]{1,0:T(8,128)(2,1)S(1)}, bf16[128,1536]{1,0:T(8,128)(2,1)S(1)}, u32[]{:S(2)}, u32[]{:S(2)}) %collective-permute-start.13) | collective-permute-done | bytes 393248 | tf_op jit(solution)/shard_map/ppermute | solution.py:14
  131.5 2.8 fusion.84
  134.3 2.6 fusion.2
  136.9 2.9 fusion.107
  141.7 3.7 fusion.117
  155.1 4.8 fusion.123
  159.9 3.7 fusion.122
  163.6 3.6 fusion.121
  167.3 3.7 fusion.120
  170.9 3.7 fusion.119
  174.7 3.8 fusion.118
  178.5 2.8 fusion.99
  181.3 18.8 %add_add_fusion = f32[2048,768]{0,1:T(8,128)} fusion(f32[2048,768]{0,1:T(8,128)} %fusion.123, f32[2048,768]{0,1:T(8,128)} %fusion.122, f32[2048,768]{0,1:T(8,128)} %fusion.121, f32[2048,768]{0,1:T(8,128)} %fusion.120, f32[2048,768]{0,1:T(8,128)} %fusion.119, f32[2048,768]{0,1:T(8,128)} %fusion.117, f32[2048,768]{0,1:T(8,128)} %fusion.118, ...), kind=kOutput, calls=%fused_computation.9 | convolution fusion | flops 413663232 | bytes 51052544 | tf_op jit(solution)/shard_map/dot_general | solution.py:66
  200.2 3.4 fusion.124
  203.6 11.5 %collective-permute-done.14 = f32[128,768]{1,0:T(8,128)S(1)} collective-permute-done((f32[128,768]{1,0:T(8,128)S(1)}, f32[128,768]{1,0:T(8,128)S(1)}, u32[]{:S(2)}, u32[]{:S(2)}) %collective-permute-start.14) | collective-permute-done | bytes 393248 | tf_op jit(solution)/shard_map/ppermute | solution.py:14
  215.1 3.3 convolution_add_fusion
  219.9 14.0 %collective-permute-done.15 = f32[128,768]{1,0:T(8,128)S(1)} collective-permute-done((f32[128,768]{1,0:T(8,128)S(1)}, f32[128,768]{1,0:T(8,128)S(1)}, u32[]{:S(2)}, u32[]{:S(2)}) %collective-permute-start.15) | collective-permute-done | bytes 393248 | tf_op jit(solution)/shard_map/ppermute | solution.py:14
  235.3 13.8 %collective-permute-done.16 = f32[128,768]{1,0:T(8,128)S(1)} collective-permute-done((f32[128,768]{1,0:T(8,128)S(1)}, f32[128,768]{1,0:T(8,128)S(1)}, u32[]{:S(2)}, u32[]{:S(2)}) %collective-permute-start.16) | collective-permute-done | bytes 393248 | tf_op jit(solution)/shard_map/ppermute | solution.py:14
  250.4 12.9 %collective-permute-done.17 = f32[128,768]{1,0:T(8,128)S(1)} collective-permute-done((f32[128,768]{1,0:T(8,128)S(1)}, f32[128,768]{1,0:T(8,128)S(1)}, u32[]{:S(2)}, u32[]{:S(2)}) %collective-permute-start.17) | collective-permute-done | bytes 393248 | tf_op jit(solution)/shard_map/ppermute | solution.py:14
  264.6 12.0 %collective-permute-done.18 = f32[128,768]{1,0:T(8,128)S(1)} collective-permute-done((f32[128,768]{1,0:T(8,128)S(1)}, f32[128,768]{1,0:T(8,128)S(1)}, u32[]{:S(2)}, u32[]{:S(2)}) %collective-permute-start.18) | collective-permute-done | bytes 393248 | tf_op jit(solution)/shard_map/ppermute | solution.py:14
  277.9 11.0 %collective-permute-done.19 = f32[128,768]{1,0:T(8,128)S(1)} collective-permute-done((f32[128,768]{1,0:T(8,128)S(1)}, f32[128,768]{1,0:T(8,128)S(1)}, u32[]{:S(2)}, u32[]{:S(2)}) %collective-permute-start.19) | collective-permute-done | bytes 393248 | tf_op jit(solution)/shard_map/ppermute | solution.py:14
  290.2 11.0 %collective-permute-done.20 = f32[128,768]{1,0:T(8,128)S(1)} collective-permute-done((f32[128,768]{1,0:T(8,128)S(1)}, f32[128,768]{1,0:T(8,128)S(1)}, u32[]{:S(2)}, u32[]{:S(2)}) %collective-permute-start.20) | collective-permute-done | bytes 393248 | tf_op jit(solution)/shard_map/ppermute | solution.py:14
  302.1 11.7 %collective-permute-done.21 = f32[128,768]{1,0:T(8,128)} collective-permute-done((f32[128,768]{1,0:T(8,128)}, f32[128,768]{1,0:T(8,128)}, u32[]{:S(2)}, u32[]{:S(2)}) %collective-permute-start.21) | collective-permute-done | bytes 393248 | tf_op jit(solution)/shard_map/ppermute | solution.py:14
  316.9 72.7 %all-reduce.3.cloned.1.call-done = f32[2048,768]{0,1:T(8,128)} async-done(((f32[2048,768]{0,1:T(8,128)}), f32[2048,768]{0,1:T(8,128)}) %all-reduce.3.cloned.1.call-update) | async-done | bytes 6291472 | tf_op jit(solution)/shard_map/psum | solution.py:74
  389.7 4.8 multiply_reduce_fusion
  400.5 23.9 %all-gather.5.cloned.1.call-done = bf16[768,768]{0,1:T(8,128)(2,1)} async-done(((bf16[768,48]{0,1:T(8,128)(2,1)}), bf16[768,768]{0,1:T(8,128)(2,1)}) %all-gather.5.cloned.1.call-update) | async-done | bytes 1179664 | tf_op jit(solution)/shard_map/all_gather | solution.py:82
  426.9 81.5 %all-reduce.5.cloned.1.call-done = f32[768,48]{0,1:T(8,128)} async-done(((f32[768,48]{0,1:T(8,128)}), f32[768,48]{0,1:T(8,128)}) %all-reduce.5.cloned.1.call-update) | async-done | bytes 147472 | tf_op jit(solution)/shard_map/psum | solution.py:86
  (144 shorter events, 42.5 us)
Async XLA Ops:
  7.2 9.0 %copy-start.19 = (bf16[128,768]{1,0:T(8,128)(2,1)S(1)}, bf16[128,768]{1,0:T(8,128)(2,1)}, u32[]{:S(2)}) copy-start(bf16[128,768]{1,0:T(8,128)(2,1)} %param.8) | copy-start | bytes 589828
  7.2 127.1 %all-gather.3.cloned.1.call-start = ((), (), s32[]{:S(2)}) async-start(), calls=%async_computation | async-start | bytes 3342336 | tf_op jit(solution)/shard_map/all_gather | solution.py:53
  11.7 378.0 %all-reduce.3.cloned.1.call-start = ((), (), s32[]{:S(2)}) async-start(), calls=%async_computation.1 | async-start | bytes 12582912 | tf_op jit(solution)/shard_map/psum | solution.py:74
  11.7 31.4 %copy-start.5 = (bf16[2048,1536]{1,0:T(8,128)(2,1)S(1)}, bf16[2048,1536]{1,0:T(8,128)(2,1)}, u32[]{:S(2)}) copy-start(bf16[2048,1536]{1,0:T(8,128)(2,1)} %param.7) | copy-start | bytes 18874372
  14.5 40.8 %collective-permute-start.1 = (bf16[128,1536]{1,0:T(8,128)(2,1)S(1)}, bf16[128,1536]{1,0:T(8,128)(2,1)S(1)}, u32[]{:S(2)}, u32[]{:S(2)}) collective-permute-start(bf16[128,1536]{1,0:T(8,128)(2,1)S(1)} %fusion.109), channel_id=1, source_target_pairs={{0,16},{16,32},{32,48},{48,64},{64,80},{80,96},{96,112},{112,0},{1... | collective-permute-start | bytes 1179656 | tf_op jit(solution)/shard_map/ppermute | solution.py:14
  16.4 17.1 %collective-permute-start = (bf16[128,768]{1,0:T(8,128)(2,1)S(1)}, bf16[128,768]{1,0:T(8,128)(2,1)S(1)}, u32[]{:S(2)}, u32[]{:S(2)}) collective-permute-start(bf16[128,768]{1,0:T(8,128)(2,1)S(1)} %fusion.116), channel_id=1, source_target_pairs={{0,16},{16,32},{32,48},{48,64},{64,80},{80,96},{96,112},{112,0},{1... | collective-permute-start | bytes 589832 | tf_op jit(solution)/shard_map/ppermute | solution.py:14
  33.5 12.5 %copy-start.21 = (bf16[128,768]{1,0:T(8,128)(2,1)}, bf16[128,768]{1,0:T(8,128)(2,1)S(1)}, u32[]{:S(2)}) copy-start(bf16[128,768]{1,0:T(8,128)(2,1)S(1)} %collective-permute-done) | copy-start | bytes 589828
  33.5 9.6 %collective-permute-start.2 = (bf16[128,768]{1,0:T(8,128)(2,1)S(1)}, bf16[128,768]{1,0:T(8,128)(2,1)S(1)}, u32[]{:S(2)}, u32[]{:S(2)}) collective-permute-start(bf16[128,768]{1,0:T(8,128)(2,1)S(1)} %collective-permute-done), channel_id=1, source_target_pairs={{0,16},{16,32},{32,48},{48,64},{64,80},{80,96},{96,112},{112,0},{1... | collective-permute-start | bytes 589832 | tf_op jit(solution)/shard_map/ppermute | solution.py:14
  43.1 9.4 %collective-permute-start.4 = (bf16[128,768]{1,0:T(8,128)(2,1)S(1)}, bf16[128,768]{1,0:T(8,128)(2,1)S(1)}, u32[]{:S(2)}, u32[]{:S(2)}) collective-permute-start(bf16[128,768]{1,0:T(8,128)(2,1)S(1)} %collective-permute-done.2), channel_id=1, source_target_pairs={{0,16},{16,32},{32,48},{48,64},{64,80},{80,96},{96,112},{112,0},{1... | collective-permute-start | bytes 589832 | tf_op jit(solution)/shard_map/ppermute | solution.py:14
  52.5 14.4 %copy-start.25 = (bf16[128,768]{1,0:T(8,128)(2,1)}, bf16[128,768]{1,0:T(8,128)(2,1)S(1)}, u32[]{:S(2)}) copy-start(bf16[128,768]{1,0:T(8,128)(2,1)S(1)} %collective-permute-done.4) | copy-start | bytes 589828
  52.5 11.5 %collective-permute-start.6 = (bf16[128,768]{1,0:T(8,128)(2,1)S(1)}, bf16[128,768]{1,0:T(8,128)(2,1)S(1)}, u32[]{:S(2)}, u32[]{:S(2)}) collective-permute-start(bf16[128,768]{1,0:T(8,128)(2,1)S(1)} %collective-permute-done.4), channel_id=1, source_target_pairs={{0,16},{16,32},{32,48},{48,64},{64,80},{80,96},{96,112},{112,0},{1... | collective-permute-start | bytes 589832 | tf_op jit(solution)/shard_map/ppermute | solution.py:14
  55.3 16.0 %collective-permute-start.3 = (bf16[128,1536]{1,0:T(8,128)(2,1)S(1)}, bf16[128,1536]{1,0:T(8,128)(2,1)S(1)}, u32[]{:S(2)}, u32[]{:S(2)}) collective-permute-start(bf16[128,1536]{1,0:T(8,128)(2,1)S(1)} %collective-permute-done.1), channel_id=1, source_target_pairs={{0,16},{16,32},{32,48},{48,64},{64,80},{80,96},{96,112},{112,0},{1... | collective-permute-start | bytes 1179656 | tf_op jit(solution)/shard_map/ppermute | solution.py:14
  64.0 13.8 %copy-start.27 = (bf16[128,768]{1,0:T(8,128)(2,1)}, bf16[128,768]{1,0:T(8,128)(2,1)S(1)}, u32[]{:S(2)}) copy-start(bf16[128,768]{1,0:T(8,128)(2,1)S(1)} %collective-permute-done.6) | copy-start | bytes 589828
  64.0 10.5 %collective-permute-start.8 = (bf16[128,768]{1,0:T(8,128)(2,1)S(1)}, bf16[128,768]{1,0:T(8,128)(2,1)S(1)}, u32[]{:S(2)}, u32[]{:S(2)}) collective-permute-start(bf16[128,768]{1,0:T(8,128)(2,1)S(1)} %collective-permute-done.6), channel_id=1, source_target_pairs={{0,16},{16,32},{32,48},{48,64},{64,80},{80,96},{96,112},{112,0},{1... | collective-permute-start | bytes 589832 | tf_op jit(solution)/shard_map/ppermute | solution.py:14
  71.3 12.9 %collective-permute-start.5 = (bf16[128,1536]{1,0:T(8,128)(2,1)S(1)}, bf16[128,1536]{1,0:T(8,128)(2,1)S(1)}, u32[]{:S(2)}, u32[]{:S(2)}) collective-permute-start(bf16[128,1536]{1,0:T(8,128)(2,1)S(1)} %collective-permute-done.3), channel_id=1, source_target_pairs={{0,16},{16,32},{32,48},{48,64},{64,80},{80,96},{96,112},{112,0},{1... | collective-permute-start | bytes 1179656 | tf_op jit(solution)/shard_map/ppermute | solution.py:14
  74.5 16.7 %copy-start.29 = (bf16[128,768]{1,0:T(8,128)(2,1)}, bf16[128,768]{1,0:T(8,128)(2,1)S(1)}, u32[]{:S(2)}) copy-start(bf16[128,768]{1,0:T(8,128)(2,1)S(1)} %collective-permute-done.8) | copy-start | bytes 589828
  74.5 13.9 %collective-permute-start.10 = (bf16[128,768]{1,0:T(8,128)(2,1)S(1)}, bf16[128,768]{1,0:T(8,128)(2,1)}, u32[]{:S(2)}, u32[]{:S(2)}) collective-permute-start(bf16[128,768]{1,0:T(8,128)(2,1)S(1)} %collective-permute-done.8), channel_id=1, source_target_pairs={{0,16},{16,32},{32,48},{48,64},{64,80},{80,96},{96,112},{112,0},{1... | collective-permute-start | bytes 589832 | tf_op jit(solution)/shard_map/ppermute | solution.py:14
  84.1 12.6 %collective-permute-start.7 = (bf16[128,1536]{1,0:T(8,128)(2,1)S(1)}, bf16[128,1536]{1,0:T(8,128)(2,1)S(1)}, u32[]{:S(2)}, u32[]{:S(2)}) collective-permute-start(bf16[128,1536]{1,0:T(8,128)(2,1)S(1)} %collective-permute-done.5), channel_id=1, source_target_pairs={{0,16},{16,32},{32,48},{48,64},{64,80},{80,96},{96,112},{112,0},{1... | collective-permute-start | bytes 1179656 | tf_op jit(solution)/shard_map/ppermute | solution.py:14
  88.4 90.0 %collective-permute-start.12 = (bf16[128,768]{1,0:T(8,128)(2,1)}, bf16[128,768]{1,0:T(8,128)(2,1)}, u32[]{:S(2)}, u32[]{:S(2)}) collective-permute-start(bf16[128,768]{1,0:T(8,128)(2,1)} %collective-permute-done.10), channel_id=1, source_target_pairs={{0,16},{16,32},{32,48},{48,64},{64,80},{80,96},{96,112},{112,0},{1... | collective-permute-start | bytes 589832 | tf_op jit(solution)/shard_map/ppermute | solution.py:14
  96.8 11.5 %collective-permute-start.9 = (bf16[128,1536]{1,0:T(8,128)(2,1)S(1)}, bf16[128,1536]{1,0:T(8,128)(2,1)S(1)}, u32[]{:S(2)}, u32[]{:S(2)}) collective-permute-start(bf16[128,1536]{1,0:T(8,128)(2,1)S(1)} %collective-permute-done.7), channel_id=1, source_target_pairs={{0,16},{16,32},{32,48},{48,64},{64,80},{80,96},{96,112},{112,0},{1... | collective-permute-start | bytes 1179656 | tf_op jit(solution)/shard_map/ppermute | solution.py:14
  108.3 11.7 %collective-permute-start.11 = (bf16[128,1536]{1,0:T(8,128)(2,1)S(1)}, bf16[128,1536]{1,0:T(8,128)(2,1)S(1)}, u32[]{:S(2)}, u32[]{:S(2)}) collective-permute-start(bf16[128,1536]{1,0:T(8,128)(2,1)S(1)} %collective-permute-done.9), channel_id=1, source_target_pairs={{0,16},{16,32},{32,48},{48,64},{64,80},{80,96},{96,112},{112,0},{1... | collective-permute-start | bytes 1179656 | tf_op jit(solution)/shard_map/ppermute | solution.py:14
  119.9 11.5 %collective-permute-start.13 = (bf16[128,1536]{1,0:T(8,128)(2,1)S(1)}, bf16[128,1536]{1,0:T(8,128)(2,1)S(1)}, u32[]{:S(2)}, u32[]{:S(2)}) collective-permute-start(bf16[128,1536]{1,0:T(8,128)(2,1)S(1)} %collective-permute-done.11), channel_id=1, source_target_pairs={{0,16},{16,32},{32,48},{48,64},{64,80},{80,96},{96,112},{112,0},{1... | collective-permute-start | bytes 1179656 | tf_op jit(solution)/shard_map/ppermute | solution.py:14
  134.3 5.5 %copy-start.31 = (f32[2048,128]{1,0:T(8,128)S(1)}, f32[2048,128]{1,0:T(8,128)}, u32[]{:S(2)}) copy-start(f32[2048,128]{1,0:T(8,128)} %fusion.98) | copy-start | bytes 3145732
  139.8 38.6 %copy-start.1 = (bf16[2048,768]{0,1:T(8,128)(2,1)}, bf16[2048,768]{0,1:T(8,128)(2,1)S(1)}, u32[]{:S(2)}) copy-start(bf16[2048,768]{0,1:T(8,128)(2,1)S(1)} %fusion.107) | copy-start | bytes 9437188
  146.7 27.9 %copy-start.7 = (bf16[2048,128]{1,0:T(8,128)(2,1)}, bf16[2048,128]{1,0:T(8,128)(2,1)S(1)}, u32[]{:S(2)}) copy-start(bf16[2048,128]{1,0:T(8,128)(2,1)S(1)} %fusion.105) | copy-start | bytes 1572868
  148.3 22.7 %copy-start.16 = (bf16[2048,128]{1,0:T(8,128)(2,1)}, bf16[2048,128]{1,0:T(8,128)(2,1)S(1)}, u32[]{:S(2)}) copy-start(bf16[2048,128]{1,0:T(8,128)(2,1)S(1)} %fusion.104) | copy-start | bytes 1572868
  149.8 17.5 %copy-start.14 = (bf16[2048,128]{1,0:T(8,128)(2,1)}, bf16[2048,128]{1,0:T(8,128)(2,1)S(1)}, u32[]{:S(2)}) copy-start(bf16[2048,128]{1,0:T(8,128)(2,1)S(1)} %fusion.103) | copy-start | bytes 1572868
  151.3 12.4 %copy-start.12 = (bf16[2048,128]{1,0:T(8,128)(2,1)}, bf16[2048,128]{1,0:T(8,128)(2,1)S(1)}, u32[]{:S(2)}) copy-start(bf16[2048,128]{1,0:T(8,128)(2,1)S(1)} %fusion.102) | copy-start | bytes 1572868
  152.7 7.2 %copy-start.10 = (bf16[2048,128]{1,0:T(8,128)(2,1)}, bf16[2048,128]{1,0:T(8,128)(2,1)S(1)}, u32[]{:S(2)}) copy-start(bf16[2048,128]{1,0:T(8,128)(2,1)S(1)} %fusion.101) | copy-start | bytes 1572868
  155.1 8.5 %copy-start.8 = (bf16[2048,128]{1,0:T(8,128)(2,1)}, bf16[2048,128]{1,0:T(8,128)(2,1)S(1)}, u32[]{:S(2)}) copy-start(bf16[2048,128]{1,0:T(8,128)(2,1)S(1)} %fusion.100) | copy-start | bytes 1572868
  200.1 224.3 %all-gather.5.cloned.1.call-start = ((), (), s32[]{:S(2)}) async-start(), calls=%async_computation.2 | async-start | bytes 1253376 | tf_op jit(solution)/shard_map/all_gather | solution.py:82
  200.2 18.6 %copy-start.2 = (bf16[2048,768]{0,1:T(8,128)(2,1)S(1)}, bf16[2048,768]{0,1:T(8,128)(2,1)}, u32[]{:S(2)}) copy-start(bf16[2048,768]{0,1:T(8,128)(2,1)} %copy-done.1) | copy-start | bytes 9437188
  200.2 18.6 %copy-start.17 = (bf16[2048,128]{1,0:T(8,128)(2,1)S(1)}, bf16[2048,128]{1,0:T(8,128)(2,1)}, u32[]{:S(2)}) copy-start(bf16[2048,128]{1,0:T(8,128)(2,1)} %copy-done.16) | copy-start | bytes 1572868
  200.2 33.9 %copy-start.15 = (bf16[2048,128]{1,0:T(8,128)(2,1)S(1)}, bf16[2048,128]{1,0:T(8,128)(2,1)}, u32[]{:S(2)}) copy-start(bf16[2048,128]{1,0:T(8,128)(2,1)} %copy-done.14) | copy-start | bytes 1572868
  203.6 11.6 %collective-permute-start.14 = (f32[128,768]{1,0:T(8,128)S(1)}, f32[128,768]{1,0:T(8,128)S(1)}, u32[]{:S(2)}, u32[]{:S(2)}) collective-permute-start(f32[128,768]{1,0:T(8,128)S(1)} %fusion.124), channel_id=1, source_target_pairs={{0,16},{16,32},{32,48},{48,64},{64,80},{80,96},{96,112},{112,0},{1... | collective-permute-start | bytes 1179656 | tf_op jit(solution)/shard_map/ppermute | solution.py:14
  218.4 30.8 %copy-start.13 = (bf16[2048,128]{1,0:T(8,128)(2,1)S(1)}, bf16[2048,128]{1,0:T(8,128)(2,1)}, u32[]{:S(2)}) copy-start(bf16[2048,128]{1,0:T(8,128)(2,1)} %copy-done.12) | copy-start | bytes 1572868
  218.4 15.6 %collective-permute-start.15 = (f32[128,768]{1,0:T(8,128)S(1)}, f32[128,768]{1,0:T(8,128)S(1)}, u32[]{:S(2)}, u32[]{:S(2)}) collective-permute-start(f32[128,768]{1,0:T(8,128)S(1)} %convolution_add_fusion), channel_id=1, source_target_pairs={{0,16},{16,32},{32,48},{48,64},{64,80},{80,96},{96,112},{112,0},{1... | collective-permute-start | bytes 1179656 | tf_op jit(solution)/shard_map/ppermute | solution.py:14
  219.9 43.5 %copy-start.11 = (bf16[2048,128]{1,0:T(8,128)(2,1)S(1)}, bf16[2048,128]{1,0:T(8,128)(2,1)}, u32[]{:S(2)}) copy-start(bf16[2048,128]{1,0:T(8,128)(2,1)} %copy-done.10) | copy-start | bytes 1572868
  234.0 15.1 %collective-permute-start.16 = (f32[128,768]{1,0:T(8,128)S(1)}, f32[128,768]{1,0:T(8,128)S(1)}, u32[]{:S(2)}, u32[]{:S(2)}) collective-permute-start(f32[128,768]{1,0:T(8,128)S(1)} %add.226), channel_id=1, source_target_pairs={{0,16},{16,32},{32,48},{48,64},{64,80},{80,96},{96,112},{112,0},{1... | collective-permute-start | bytes 1179656 | tf_op jit(solution)/shard_map/ppermute | solution.py:14
  235.3 41.4 %copy-start.9 = (bf16[2048,128]{1,0:T(8,128)(2,1)S(1)}, bf16[2048,128]{1,0:T(8,128)(2,1)}, u32[]{:S(2)}) copy-start(bf16[2048,128]{1,0:T(8,128)(2,1)} %copy-done.8) | copy-start | bytes 1572868
  249.1 14.2 %collective-permute-start.17 = (f32[128,768]{1,0:T(8,128)S(1)}, f32[128,768]{1,0:T(8,128)S(1)}, u32[]{:S(2)}, u32[]{:S(2)}) collective-permute-start(f32[128,768]{1,0:T(8,128)S(1)} %add.227), channel_id=1, source_target_pairs={{0,16},{16,32},{32,48},{48,64},{64,80},{80,96},{96,112},{112,0},{1... | collective-permute-start | bytes 1179656 | tf_op jit(solution)/shard_map/ppermute | solution.py:14
  250.4 38.6 %copy-start.20 = (bf16[2048,128]{1,0:T(8,128)(2,1)S(1)}, bf16[2048,128]{1,0:T(8,128)(2,1)}, u32[]{:S(2)}) copy-start(bf16[2048,128]{1,0:T(8,128)(2,1)} %fusion.99) | copy-start | bytes 1572868
  263.3 13.2 %collective-permute-start.18 = (f32[128,768]{1,0:T(8,128)S(1)}, f32[128,768]{1,0:T(8,128)S(1)}, u32[]{:S(2)}, u32[]{:S(2)}) collective-permute-start(f32[128,768]{1,0:T(8,128)S(1)} %add.228), channel_id=1, source_target_pairs={{0,16},{16,32},{32,48},{48,64},{64,80},{80,96},{96,112},{112,0},{1... | collective-permute-start | bytes 1179656 | tf_op jit(solution)/shard_map/ppermute | solution.py:14
  276.6 12.3 %collective-permute-start.19 = (f32[128,768]{1,0:T(8,128)S(1)}, f32[128,768]{1,0:T(8,128)S(1)}, u32[]{:S(2)}, u32[]{:S(2)}) collective-permute-start(f32[128,768]{1,0:T(8,128)S(1)} %add.229), channel_id=1, source_target_pairs={{0,16},{16,32},{32,48},{48,64},{64,80},{80,96},{96,112},{112,0},{1... | collective-permute-start | bytes 1179656 | tf_op jit(solution)/shard_map/ppermute | solution.py:14
  288.9 12.3 %collective-permute-start.20 = (f32[128,768]{1,0:T(8,128)S(1)}, f32[128,768]{1,0:T(8,128)S(1)}, u32[]{:S(2)}, u32[]{:S(2)}) collective-permute-start(f32[128,768]{1,0:T(8,128)S(1)} %add.230), channel_id=1, source_target_pairs={{0,16},{16,32},{32,48},{48,64},{64,80},{80,96},{96,112},{112,0},{1... | collective-permute-start | bytes 1179656 | tf_op jit(solution)/shard_map/ppermute | solution.py:14
  302.0 11.8 %collective-permute-start.21 = (f32[128,768]{1,0:T(8,128)}, f32[128,768]{1,0:T(8,128)}, u32[]{:S(2)}, u32[]{:S(2)}) collective-permute-start(f32[128,768]{1,0:T(8,128)} %add.231), channel_id=1, source_target_pairs={{0,16},{16,32},{32,48},{48,64},{64,80},{80,96},{96,112},{112,0},{1... | collective-permute-start | bytes 1179656 | tf_op jit(solution)/shard_map/ppermute | solution.py:14
  302.1 206.4 %all-reduce.5.cloned.1.call-start = ((), (), s32[]{:S(2)}) async-start(), calls=%async_computation.3 | async-start | bytes 294912 | tf_op jit(solution)/shard_map/psum | solution.py:86
  389.7 6.5 %copy-start.4 = (f32[2048,768]{0,1:T(8,128)S(1)}, f32[2048,768]{0,1:T(8,128)}, u32[]{:S(2)}) copy-start(f32[2048,768]{0,1:T(8,128)} %all-reduce.3.cloned.1.call-done) | copy-start | bytes 18874372
  (17 other events, 35.0 us)
Sparse Core Ops, SparseCore 0:
  11.8 103.8 all-gather.2
  200.2 189.4 all-reduce.2
  391.4 33.0 all-gather.4
  427.4 81.0 all-reduce.4
where the time goes:
time: 525 us; the launch traced here: 517 us
  waiting for transfers between devices  362 us (69%)
  matrix products  100 us (19%)
  other arithmetic  25.8 us (5%)
  between operations  14.7 us (3%)
  local copies, waits for them, and re-layouts  9.35 us (2%)
    ppermute x22, waiting for transfers between devices, passed_along(): return lax.ppermute(value, axis, pairs)  184 us
    psum x1, waiting for transfers between devices, per_device(): grad_head = lax.psum(head_part, 'dp')  81.5 us
    psum x1, waiting for transfers between devices, per_device(): summed = lax.psum(img_grads, 'tensor')  72.7 us
    dot_general x8, matrix products, per_device(): jnp.dot(coef, travel_emb, preferred_element_type=jnp.float32)  45.8 us
    all_gather x1, waiting for transfers between devices, per_device(): head_full = lax.all_gather(head, 'tensor', axis=1, tiled=True)  23.9 us
    dot_general x8, matrix products, affinity_tile(): lax.dot_general(tea_img_emb, tea_piece, contract, preferred_element_type=...  22.6 us
    dot_general x8, matrix products, transpose_product(): lax.dot_general(coef, img_emb, (((0,), (0,)), ((), ())), preferred_elemen...  13.6 us
    dot_general x8, matrix products, affinity_tile(): lax.dot_general(img_emb, txt_piece, contract, preferred_element_type=jnp....  11.8 us
  transfers between devices with their start and end apart: 26, of which 23 were waited for; matrix products, arithmetic and copies ran while one was open for 20% of the time, Pallas kernels for 0%

commit v1 on v0

v1 whole, which is shorter than its diff:
```python
import functools

import jax
import jax.numpy as jnp
from jax import lax
from jax.experimental import pallas as pl
from jax.experimental.pallas import tpu as pltpu
from jax.sharding import PartitionSpec as P

logit_scale = 64.0
logit_bias = -2.0
loss_scale = 65536.0

F32 = jnp.float32
BF16 = jnp.bfloat16
MESH = pl.DeviceIdType.MESH
NT = (((1,), (1,)), ((), ()))
NN = (((1,), (0,)), ((), ()))
EPS = 1e-06


def dot(a, b, dims=NN):
    return lax.dot_general(a, b, dims, preferred_element_type=F32)


def unit_of(values):
    floats = values.astype(F32)
    length = jnp.sqrt(jnp.sum(floats * floats, axis=1, keepdims=True) + EPS)
    inverse = 1.0 / length
    return floats * inverse, inverse


def kernel(
    factor,
    images_hbm,
    head_ref,
    tea_hbm,
    txt_hbm,
    teatxt_hbm,
    gi_ref,
    gh_ref,
    gt_ref,
    images,
    tea,
    rawtxt,
    rawtea,
    headg,
    img,
    img_t,
    tbuf,
    gimg,
    gacc,
    gown,
    gstage,
    grecv,
    pstage,
    precv,
    rstage,
    rrecv,
    rown,
    unit_own,
    inv_own,
    astage,
    arecv,
    xstage,
    xrecv,
    ystage,
    yrecv,
    lsem,
    hsend,
    hrecv,
    tsend,
    trecv,
    gsend,
    gsem,
    psend,
    psem,
    rsend,
    rsem,
    asend,
    asem,
    xsend,
    xsem,
    ysend,
    ysem,
):
    me_dp = lax.axis_index("dp")
    me_t = lax.axis_index("tensor")
    y_hi = me_dp // 4
    x = me_dp % 4
    chip = me_t // 2
    core = me_t % 2
    y_lo = me_t // 8
    flip_t = (1 - y_lo) * 8 + me_t % 8
    mate = chip * 2 + (1 - core)

    def at_x(dx):
        return y_hi * 4 + lax.rem(x + dx, 4)

    def across_x(dx):
        return (1 - y_hi) * 4 + lax.rem(x + dx, 4)

    def group(dx, side):
        if side == 0:
            return (at_x(dx), me_t)
        return (across_x(dx), flip_t)

    def plane(j):
        return (me_dp, lax.rem(chip + j, 8) * 2 + core)

    def remote(src, dst, ssem, rsem_, device):
        return pltpu.make_async_remote_copy(
            src_ref=src, dst_ref=dst, send_sem=ssem, recv_sem=rsem_, device_id=device, device_id_type=MESH
        )

    loads = [
        pltpu.make_async_copy(txt_hbm, rawtxt, lsem.at[0]),
        pltpu.make_async_copy(teatxt_hbm, rawtea, lsem.at[1]),
        pltpu.make_async_copy(tea_hbm, tea, lsem.at[2]),
        pltpu.make_async_copy(images_hbm, images, lsem.at[3]),
    ]
    for load in loads:
        load.start()

    partners = [group(dx, side) for dx in range(4) for side in range(2) if (dx, side) != (0, 0)]
    partners += [(me_dp, lax.rem(me_t + j, 16)) for j in range(1, 16)]
    partners += [((1 - y_hi) * 4 + x, me_t)]
    barrier = pltpu.get_barrier_semaphore()
    for device in partners:
        pl.semaphore_signal(barrier, inc=1, device_id=device, device_id_type=MESH)

    loads[0].wait()
    tbuf[0, 0, :, 0:768] = unit_of(rawtxt[...])[0].astype(BF16)
    loads[1].wait()
    tbuf[0, 0, :, 768:2304] = unit_of(rawtea[...])[0].astype(BF16)
    headg[chip, core] = head_ref[...]

    pl.semaphore_wait(barrier, len(partners))

    sends = []

    own = tbuf.at[0, 0]
    first = [
        remote(own, tbuf.at[0, 1], tsend.at[0], trecv.at[0], group(0, 1)),
        remote(own, tbuf.at[1, 1], tsend.at[1], trecv.at[2], group(1, 0)),
        remote(own, tbuf.at[1, 0], tsend.at[2], trecv.at[1], group(3, 0)),
    ]
    for copy in first:
        copy.start()
    sends += first

    heads = [
        remote(head_ref, headg.at[chip, core], hsend.at[j - 1], hrecv.at[chip], plane(j)) for j in range(1, 8)
    ]
    for copy in heads:
        copy.start()
    sends += heads

    loads[2].wait()

    @pl.loop(0, 32)
    def _(i):
        rows = pl.ds(pl.multiple_of(i * 64, 64), 64)
        tea[rows, :] = unit_of(tea[rows, :])[0].astype(BF16)

    for j in range(1, 8):
        other = lax.rem(chip + j, 8)
        remote(head_ref, headg.at[other, core], hsend.at[j - 1], hrecv.at[other], plane(j)).wait_recv()
    to_mate = remote(headg.at[:, core], headg.at[:, core], hsend.at[7], hrecv.at[8], (me_dp, mate))
    to_mate.start()
    sends.append(to_mate)
    loads[3].wait()
    remote(headg.at[:, 1 - core], headg.at[:, 1 - core], hsend.at[7], hrecv.at[8], (me_dp, mate)).wait_recv()

    def head_all():
        return headg[...].reshape(768, 768)

    @pl.loop(0, 8)
    def _(r):
        rows = pl.ds(pl.multiple_of(r * 256, 256), 256)
        proj = dot(images[rows, :], head_all(), NT).astype(BF16)
        unit = unit_of(proj)[0]
        img[rows, :] = unit.astype(BF16)
        img_t[r] = unit.T.astype(BF16)

    own_rows = pl.ds(pl.multiple_of(me_t * 128, 128), 128)
    unit, inverse = unit_of(dot(images[own_rows, :], head_all(), NT).astype(BF16))
    unit_own[...] = unit
    inv_own[...] = inverse

    def chunk(pair, r):
        rows = pl.ds(pl.multiple_of(r * 256, 256), 256)
        block = tbuf[pair].reshape(256, 2304)
        txt = block[:, 0:768]
        target = dot(tea[rows, :], block[:, 768:2304], NT)
        student = dot(img[rows, :], txt, NT)
        half = 0.5 * logit_scale
        coef = (
            (jnp.tanh(half * student + 0.5 * logit_bias) - jnp.tanh(half * target + 0.5 * logit_bias))
            * (0.5 * factor)
        ).astype(BF16)
        part = dot(coef, txt)
        if pair == 0:
            gimg[rows, :] = part
        else:
            gimg[rows, :] += part
        gacc[...] += dot(img_t[r], coef)

    def begin_step():
        gacc[...] = jnp.zeros_like(gacc)

    def wait_text(slot, pair, k, rows=None):
        ref = tbuf.at[pair, k] if rows is None else tbuf.at[pair, k, rows]
        remote(ref, ref, tsend.at[0], trecv.at[slot], group(0, 1)).wait_recv()

    def forward(src, dst, send, slot, device):
        copy = remote(src, dst, tsend.at[send], trecv.at[slot], device)
        copy.start()
        sends.append(copy)

    low, high = pl.ds(0, 64), pl.ds(64, 64)

    def send_text_grad(pair, k, device):
        index = pair * 2 + k
        mirror = {(0, 1): (0, 1), (1, 0): (1, 1), (1, 1): (1, 0), (2, 0): (2, 1), (2, 1): (2, 0), (3, 0): (3, 0), (3, 1): (3, 1)}
        there = mirror[(pair, k)]
        copy = remote(
            gstage.at[pair, k],
            grecv.at[there[0], there[1]],
            gsend.at[index],
            gsem.at[there[0] * 2 + there[1]],
            device,
        )
        copy.start()
        sends.append(copy)

    def stage_text_grads(pair):
        if pair == 0:
            gown[...] = gacc[:, 0:128]
        else:
            gstage[pair, 0] = gacc[:, 0:128].astype(BF16)
        gstage[pair, 1] = gacc[:, 128:256].astype(BF16)

    wait_text(0, 0, 1)
    forward(tbuf.at[0, 1], tbuf.at[2, 1], 3, 4, group(1, 0))
    forward(tbuf.at[0, 1], tbuf.at[2, 0], 4, 3, group(3, 0))
    wait_text(2, 1, 1)
    forward(tbuf.at[1, 1, low], tbuf.at[3, 0, low], 5, 5, group(1, 0))
    wait_text(1, 1, 0)
    forward(tbuf.at[1, 0, high], tbuf.at[3, 0, high], 6, 6, group(3, 0))
    begin_step()

    @pl.loop(0, 8)
    def _(r):
        chunk(0, r)

    stage_text_grads(0)
    send_text_grad(0, 1, group(0, 1))

    begin_step()

    @pl.loop(0, 8)
    def _(r):
        chunk(1, r)

    stage_text_grads(1)

    wait_text(4, 2, 1)
    forward(tbuf.at[2, 1, low], tbuf.at[3, 1, low], 7, 7, group(1, 0))
    wait_text(3, 2, 0)
    forward(tbuf.at[2, 0, high], tbuf.at[3, 1, high], 8, 8, group(3, 0))
    send_text_grad(1, 0, group(1, 0))
    send_text_grad(1, 1, group(3, 0))
    begin_step()

    @pl.loop(0, 8)
    def _(r):
        chunk(2, r)

    stage_text_grads(2)

    wait_text(5, 3, 0, low)
    wait_text(6, 3, 0, high)
    wait_text(7, 3, 1, low)
    wait_text(8, 3, 1, high)
    send_text_grad(2, 0, group(1, 1))
    send_text_grad(2, 1, group(3, 1))
    begin_step()

    def owner(k):
        return lax.rem(chip + 1 + k, 8)

    def from_mate(k):
        return remote(pstage.at[k], precv.at[k], psend.at[k], psem.at[k], (me_dp, mate))

    def to_owner(k):
        return remote(rstage.at[k], rrecv.at[chip], rsend.at[k], rsem.at[chip], (me_dp, owner(k) * 2 + core))

    def chip_sum(k):
        mine = pl.ds(pl.multiple_of(owner(k) * 256 + core * 128, 128), 128)
        from_mate(k).wait_recv()
        return gimg[mine, :] + precv[k].astype(F32)

    @pl.loop(0, 8)
    def _(k):
        r = owner(k)
        chunk(3, r)
        theirs = pl.ds(pl.multiple_of(r * 256 + (1 - core) * 128, 128), 128)
        pstage[k] = gimg[theirs, :].astype(BF16)
        from_mate(k).start()

        @pl.when(k > 0)
        def _():
            rstage[k - 1] = chip_sum(k - 1).astype(BF16)
            to_owner(k - 1).start()

    stage_text_grads(3)
    send_text_grad(3, 0, group(2, 0))
    send_text_grad(3, 1, group(2, 1))

    rown[...] = chip_sum(7)
    for j in range(1, 8):
        other = lax.rem(chip + j, 8)
        remote(rstage.at[0], rrecv.at[other], rsend.at[0], rsem.at[other], plane(j)).wait_recv()
        rown[...] += rrecv[other].astype(F32)

    total = rown[...]
    unit = unit_own[...]
    row_dot = jnp.sum(unit * total, axis=1, keepdims=True)
    grad_proj = (total - unit * row_dot) * inv_own[...]
    astage[...] = grad_proj.T.astype(BF16).reshape(16, 48, 128)
    arecv[me_t] = astage[me_t]
    scatter = []
    for j in range(1, 16):
        other = lax.rem(me_t + j, 16)
        copy = remote(astage.at[other], arecv.at[me_t], asend.at[j - 1], asem.at[me_t], (me_dp, other))
        copy.start()
        scatter.append(copy)
    sends += scatter

    gi_ref[...] = dot(grad_proj.astype(BF16), head_all())

    for j in range(1, 16):
        other = lax.rem(me_t + j, 16)
        remote(astage.at[other], arecv.at[other], asend.at[j - 1], asem.at[other], (me_dp, other)).wait_recv()

    head_part = jnp.zeros((48, 768), F32)
    for s in range(8):
        pieces = jnp.concatenate([arecv[2 * s], arecv[2 * s + 1]], axis=1)
        head_part += dot(pieces, images[s * 256 : (s + 1) * 256, :])
    xstage[...] = head_part.astype(BF16)
    xrecv[x] = xstage[...]
    for j in range(1, 4):
        copy = remote(xstage, xrecv.at[x], xsend.at[j - 1], xsem.at[x], (at_x(j), me_t))
        copy.start()
        sends.append(copy)

    text_sum = gown[...]
    for pair in range(4):
        for k in range(2):
            if (pair, k) != (0, 0):
                remote(
                    gstage.at[pair, k], grecv.at[pair, k], gsend.at[0], gsem.at[pair * 2 + k], group(0, 1)
                ).wait_recv()
                text_sum = text_sum + grecv[pair, k].astype(F32)
    text_grad = text_sum.T
    unit, inverse = unit_of(rawtxt[...])
    gt_ref[...] = (text_grad - unit * jnp.sum(unit * text_grad, axis=1, keepdims=True)) * inverse

    for j in range(1, 4):
        other = lax.rem(x + j, 4)
        remote(xstage, xrecv.at[other], xsend.at[j - 1], xsem.at[other], (at_x(j), me_t)).wait_recv()
    ystage[...] = (
        (xrecv[0].astype(F32) + xrecv[1].astype(F32)) + (xrecv[2].astype(F32) + xrecv[3].astype(F32))
    ).astype(BF16)
    swap = remote(ystage, yrecv, ysend.at[0], ysem.at[0], ((1 - y_hi) * 4 + x, me_t))
    swap.start()
    swap.wait_recv()
    sends.append(swap)
    gh_ref[...] = ystage[...].astype(F32) + yrecv[...].astype(F32)

    for copy in sends:
        copy.wait_send()

    @pl.loop(0, 8)
    def _(k):
        from_mate(k).wait_send()

        @pl.when(k < 7)
        def _():
            to_owner(k).wait_send()


def per_device(images, head, tea_img, stu_txt, tea_txt):
    factor = logit_scale * loss_scale / (images.shape[0] * lax.axis_size("dp"))
    any_spec = pl.BlockSpec(memory_space=pl.ANY)
    vmem_spec = pl.BlockSpec(memory_space=pltpu.VMEM)
    dma = pltpu.SemaphoreType.DMA
    grad_images, grad_head, grad_text = pl.pallas_call(
        functools.partial(kernel, factor),
        name="distill",
        out_shape=(
            jax.ShapeDtypeStruct((128, 768), F32),
            jax.ShapeDtypeStruct((48, 768), F32),
            jax.ShapeDtypeStruct((128, 768), F32),
        ),
        in_specs=[any_spec, vmem_spec, any_spec, any_spec, any_spec],
        out_specs=(vmem_spec, vmem_spec, vmem_spec),
        scratch_shapes=[
            pltpu.VMEM((2048, 768), BF16),
            pltpu.VMEM((2048, 1536), BF16),
            pltpu.VMEM((128, 768), BF16),
            pltpu.VMEM((128, 1536), BF16),
            pltpu.VMEM((8, 2, 48, 768), BF16),
            pltpu.VMEM((2048, 768), BF16),
            pltpu.VMEM((8, 768, 256), BF16),
            pltpu.VMEM((4, 2, 128, 2304), BF16),
            pltpu.VMEM((2048, 768), F32),
            pltpu.VMEM((768, 256), F32),
            pltpu.VMEM((768, 128), F32),
            pltpu.VMEM((4, 2, 768, 128), BF16),
            pltpu.VMEM((4, 2, 768, 128), BF16),
            pltpu.VMEM((8, 128, 768), BF16),
            pltpu.VMEM((8, 128, 768), BF16),
            pltpu.VMEM((8, 128, 768), BF16),
            pltpu.VMEM((8, 128, 768), BF16),
            pltpu.VMEM((128, 768), F32),
            pltpu.VMEM((128, 768), F32),
            pltpu.VMEM((128, 1), F32),
            pltpu.VMEM((16, 48, 128), BF16),
            pltpu.VMEM((16, 48, 128), BF16),
            pltpu.VMEM((48, 768), BF16),
            pltpu.VMEM((4, 48, 768), BF16),
            pltpu.VMEM((48, 768), BF16),
            pltpu.VMEM((48, 768), BF16),
            dma((4,)),
            dma((8,)),
            dma((9,)),
            dma((9,)),
            dma((9,)),
            dma((8,)),
            dma((8,)),
            dma((8,)),
            dma((8,)),
            dma((8,)),
            dma((8,)),
            dma((15,)),
            dma((16,)),
            dma((3,)),
            dma((4,)),
            dma((1,)),
            dma((1,)),
        ],
        compiler_params=pltpu.CompilerParams(
            collective_id=0, has_side_effects=True, vmem_limit_bytes=60 * 1024 * 1024
        ),
    )(images, head.T, tea_img, stu_txt, tea_txt)
    return (grad_images, grad_head.T, grad_text)


def solution(mesh):
    placed = (
        P("dp", None),
        P(None, "tensor"),
        P("dp", None),
        P(("dp", "tensor"), None),
        P(("dp", "tensor"), None),
    )
    return jax.shard_map(
        per_device,
        mesh=mesh,
        in_specs=placed,
        out_specs=(P(("dp", "tensor"), None), P(None, "tensor"), P(("dp", "tensor"), None)),
        check_vma=False,
    )
```

time: 525 us -> 110 us (0.21); the launches traced: 517 us -> 109 us
  waiting for transfers between devices: 362 us -> 0 us
  Pallas kernels: 0 us -> 104 us
  matrix products: 100 us -> 0 us
  other arithmetic: 25.8 us -> 0 us
  between operations: 14.7 us -> 0.64 us
    ppermute x22 -> x0, waiting for transfers between devices: 184 us -> none  [passed_along(): return lax.ppermute(value, axis, pairs)]
    psum x2 -> x0, waiting for transfers between devices: 154 us -> none  [the longest x1 81.5 us: per_device(): grad_head = lax.psum(head_part, 'dp')]
    pallas_call x0 -> x1, Pallas kernels: none -> 104 us  [per_device(): pl.pallas_call(functools.partial(kernel, factor), name='distill', out_sha...]
    dot_general x35 -> x0, matrix products: 100 us -> none  [the longest x8 45.8 us: per_device(): jnp.dot(coef, travel_emb, preferred_element_type=jnp.float32)]
    all_gather x2 -> x0, waiting for transfers between devices: 23.9 us -> none  [the longest x1 23.9 us: per_device(): head_full = lax.all_gather(head, 'tensor', axis=1, tiled=True)]
    reduce_sum x6 -> x0, other arithmetic: 14.1 us -> none  [the longest x4 8.16 us: normalize(): length = jnp.sqrt(jnp.sum(floats * floats, axis=1, keepdims=True) + 1e-06)]
    convert_element_type x5 -> x0, other arithmetic: 8.73 us -> none  [the longest x1 2.89 us: per_device(): tea_img_emb = normalize(tea_img)[0].astype(jnp.bfloat16)]
  transfers between devices with their start and end apart: 26 -> 0, of which waited for: 23 -> 0; matrix products, arithmetic and copies ran while one was open for 20% -> 0% of each run, Pallas kernels for 0% -> 0%
where the time goes in v1:
time: 110 us; the launch traced here: 109 us
  Pallas kernels  104 us (95%)
  local copies, waits for them, and re-layouts  5.11 us (5%)
    pallas_call x1, Pallas kernels, per_device(): pl.pallas_call(functools.partial(kernel, factor), name='distill', out_sha...  104 us
    unnamed x3, local copies, waits for them, and re-layouts  5.11 us

profile of v1, /device:TPU:0, one launch (start us, length us, event | category | flops | bytes accessed | tf_op | source)
XLA Modules:
  0.0 109.4 jit_solution(16469420280148756674)
XLA Ops:
  0.6 103.7 %distill.1 = (f32[128,768]{1,0:T(8,128)}, f32[48,768]{1,0:T(8,128)}, f32[128,768]{1,0:T(8,128)}) custom-call(bf16[2048,768]{1,0:T(8,128)(2,1)} %images_hbm.1, bf16[48,768]{1,0:T(8,128)(2,1)} %bitcast.3, bf16[2048,1536]{1,0:T(8,128)(2,1)} %tea_hbm.1, bf16[128,768]{1,0:T(8,128)(2,1)} %txt_hbm.1, bf16[128,1536]{1,0:T(8,128)(2,1)} %teatxt_hbm.1), custom_call_target="tpu_custom_call" | custom-call | tf_op jit(solution)/shard_map/distill/pallas_call | solution.py:399
  104.3 1.8 %copy.11 = f32[128,768]{1,0:T(8,128)} copy(f32[128,768]{1,0:T(8,128)} %get-tuple-element.12) | data formatting | bytes 786432
  106.1 1.6 %copy.12 = f32[768,48]{0,1:T(8,128)} copy(f32[768,48]{0,1:T(8,128)} %bitcast.2) | data formatting | bytes 294912
  107.6 1.8 %copy.13 = f32[128,768]{1,0:T(8,128)} copy(f32[128,768]{1,0:T(8,128)} %get-tuple-element.14) | data formatting | bytes 786432

commit v2 on v1

--- a/solution.py
+++ b/solution.py
@@ -130,24 +130,46 @@
         pl.semaphore_signal(barrier, inc=1, device_id=device, device_id_type=MESH)
 
     loads[0].wait()
-    tbuf[0, 0, :, 0:768] = unit_of(rawtxt[...])[0].astype(BF16)
+    tbuf[0, 0:128, 0:768] = unit_of(rawtxt[...])[0].astype(BF16)
     loads[1].wait()
-    tbuf[0, 0, :, 768:2304] = unit_of(rawtea[...])[0].astype(BF16)
+    tbuf[0, 0:128, 768:2304] = unit_of(rawtea[...])[0].astype(BF16)
     headg[chip, core] = head_ref[...]
 
     pl.semaphore_wait(barrier, len(partners))
 
     sends = []
 
-    own = tbuf.at[0, 0]
-    first = [
-        remote(own, tbuf.at[0, 1], tsend.at[0], trecv.at[0], group(0, 1)),
-        remote(own, tbuf.at[1, 1], tsend.at[1], trecv.at[2], group(1, 0)),
-        remote(own, tbuf.at[1, 0], tsend.at[2], trecv.at[1], group(3, 0)),
+    places = [
+        (0, 128), (0, 192),
+        (1, 0), (1, 64),
+        (1, 128), (1, 192),
+        (2, 0), (2, 64),
+        (2, 128), (3, 64),
+        (3, 0), (2, 192),
+        (3, 128), (3, 192),
     ]
-    for copy in first:
+
+    def text_at(place):
+        return tbuf.at[place[0], pl.ds(place[1], 64)]
+
+    def send_text(src, index, send, device):
+        copy = remote(text_at(src), text_at(places[index]), tsend.at[send], trecv.at[index], device)
         copy.start()
-    sends += first
+        sends.append(copy)
+
+    def wait_text(*indices):
+        for index in indices:
+            ref = text_at(places[index])
+            remote(ref, ref, tsend.at[0], trecv.at[index], across).wait_recv()
+
+    across, ahead, behind = group(0, 1), group(1, 0), group(3, 0)
+    own_low, own_high = (0, 0), (0, 64)
+    send_text(own_low, 0, 0, across)
+    send_text(own_low, 4, 1, ahead)
+    send_text(own_high, 3, 2, behind)
+    send_text(own_high, 1, 3, across)
+    send_text(own_high, 5, 4, ahead)
+    send_text(own_low, 2, 5, behind)
 
     heads = [
         remote(head_ref, headg.at[chip, core], hsend.at[j - 1], hrecv.at[chip], plane(j)) for j in range(1, 8)
@@ -175,117 +197,101 @@
     def head_all():
         return headg[...].reshape(768, 768)
 
-    @pl.loop(0, 8)
-    def _(r):
+    def project(r):
         rows = pl.ds(pl.multiple_of(r * 256, 256), 256)
         proj = dot(images[rows, :], head_all(), NT).astype(BF16)
         unit = unit_of(proj)[0]
         img[rows, :] = unit.astype(BF16)
         img_t[r] = unit.T.astype(BF16)
 
+    @pl.loop(0, 4)
+    def _(r):
+        project(r)
+
+    wait_text(4, 3)
+    send_text(places[4], 6, 6, ahead)
+    send_text(places[3], 7, 7, behind)
+
+    @pl.loop(4, 8)
+    def _(r):
+        project(r)
+
     own_rows = pl.ds(pl.multiple_of(me_t * 128, 128), 128)
     unit, inverse = unit_of(dot(images[own_rows, :], head_all(), NT).astype(BF16))
     unit_own[...] = unit
     inv_own[...] = inverse
 
-    def chunk(pair, r):
+    def coef_of(step, r):
         rows = pl.ds(pl.multiple_of(r * 256, 256), 256)
-        block = tbuf[pair].reshape(256, 2304)
-        txt = block[:, 0:768]
-        target = dot(tea[rows, :], block[:, 768:2304], NT)
-        student = dot(img[rows, :], txt, NT)
+        target = dot(tea[rows, :], tbuf[step, :, 768:2304], NT)
+        student = dot(img[rows, :], tbuf[step, :, 0:768], NT)
         half = 0.5 * logit_scale
-        coef = (
+        return (
             (jnp.tanh(half * student + 0.5 * logit_bias) - jnp.tanh(half * target + 0.5 * logit_bias))
             * (0.5 * factor)
         ).astype(BF16)
-        part = dot(coef, txt)
-        if pair == 0:
+
+    def grads_of(step, r, coef, first):
+        rows = pl.ds(pl.multiple_of(r * 256, 256), 256)
+        part = dot(coef, tbuf[step, :, 0:768])
+        if step == 0:
             gimg[rows, :] = part
         else:
             gimg[rows, :] += part
-        gacc[...] += dot(img_t[r], coef)
-
-    def begin_step():
-        gacc[...] = jnp.zeros_like(gacc)
-
-    def wait_text(slot, pair, k, rows=None):
-        ref = tbuf.at[pair, k] if rows is None else tbuf.at[pair, k, rows]
-        remote(ref, ref, tsend.at[0], trecv.at[slot], group(0, 1)).wait_recv()
-
-    def forward(src, dst, send, slot, device):
-        copy = remote(src, dst, tsend.at[send], trecv.at[slot], device)
-        copy.start()
-        sends.append(copy)
-
-    low, high = pl.ds(0, 64), pl.ds(64, 64)
-
-    def send_text_grad(pair, k, device):
-        index = pair * 2 + k
-        mirror = {(0, 1): (0, 1), (1, 0): (1, 1), (1, 1): (1, 0), (2, 0): (2, 1), (2, 1): (2, 0), (3, 0): (3, 0), (3, 1): (3, 1)}
-        there = mirror[(pair, k)]
+        text_part = dot(img_t[r], coef)
+        if first:
+            gacc[...] = text_part
+        else:
+            gacc[...] += text_part
+
+    def run_step(step):
+        coef = coef_of(step, 0)
+        for r in range(8):
+            later = coef_of(step, r + 1) if r < 7 else None
+            grads_of(step, r, coef, r == 0)
+            coef = later
+
+    owners = [None, across, ahead, behind, group(2, 0), group(3, 1), group(1, 1), group(2, 1)]
+    mirror = [0, 1, 3, 2, 4, 6, 5, 7]
+
+    def send_text_grad(block):
         copy = remote(
-            gstage.at[pair, k],
-            grecv.at[there[0], there[1]],
-            gsend.at[index],
-            gsem.at[there[0] * 2 + there[1]],
-            device,
+            gstage.at[block],
+            grecv.at[mirror[block]],
+            gsend.at[block],
+            gsem.at[mirror[block]],
+            owners[block],
         )
         copy.start()
         sends.append(copy)
 
-    def stage_text_grads(pair):
-        if pair == 0:
-            gown[...] = gacc[:, 0:128]
-        else:
-            gstage[pair, 0] = gacc[:, 0:128].astype(BF16)
-        gstage[pair, 1] = gacc[:, 128:256].astype(BF16)
-
-    wait_text(0, 0, 1)
-    forward(tbuf.at[0, 1], tbuf.at[2, 1], 3, 4, group(1, 0))
-    forward(tbuf.at[0, 1], tbuf.at[2, 0], 4, 3, group(3, 0))
-    wait_text(2, 1, 1)
-    forward(tbuf.at[1, 1, low], tbuf.at[3, 0, low], 5, 5, group(1, 0))
-    wait_text(1, 1, 0)
-    forward(tbuf.at[1, 0, high], tbuf.at[3, 0, high], 6, 6, group(3, 0))
-    begin_step()
-
-    @pl.loop(0, 8)
-    def _(r):
-        chunk(0, r)
-
-    stage_text_grads(0)
-    send_text_grad(0, 1, group(0, 1))
-
-    begin_step()
-
-    @pl.loop(0, 8)
-    def _(r):
-        chunk(1, r)
-
-    stage_text_grads(1)
-
-    wait_text(4, 2, 1)
-    forward(tbuf.at[2, 1, low], tbuf.at[3, 1, low], 7, 7, group(1, 0))
-    wait_text(3, 2, 0)
-    forward(tbuf.at[2, 0, high], tbuf.at[3, 1, high], 8, 8, group(3, 0))
-    send_text_grad(1, 0, group(1, 0))
-    send_text_grad(1, 1, group(3, 0))
-    begin_step()
-
-    @pl.loop(0, 8)
-    def _(r):
-        chunk(2, r)
-
-    stage_text_grads(2)
-
-    wait_text(5, 3, 0, low)
-    wait_text(6, 3, 0, high)
-    wait_text(7, 3, 1, low)
-    wait_text(8, 3, 1, high)
-    send_text_grad(2, 0, group(1, 1))
-    send_text_grad(2, 1, group(3, 1))
-    begin_step()
+    wait_text(0, 1)
+    send_text(places[0], 8, 8, ahead)
+    send_text(places[1], 11, 9, behind)
+    send_text(places[1], 9, 10, ahead)
+    send_text(places[0], 10, 11, behind)
+    run_step(0)
+    gown[...] = gacc[:, 0:128]
+    gstage[1] = gacc[:, 128:256].astype(BF16)
+    send_text_grad(1)
+
+    wait_text(2, 5)
+    run_step(1)
+    gstage[2] = gacc[:, 0:128].astype(BF16)
+    gstage[3] = gacc[:, 128:256].astype(BF16)
+
+    wait_text(6, 7)
+    send_text(places[6], 12, 12, across)
+    send_text(places[7], 13, 13, across)
+    wait_text(8, 11)
+    run_step(2)
+    gstage[4] = gacc[:, 0:128].astype(BF16)
+    gstage[5, :, 0:64] = gacc[:, 128:192].astype(BF16)
+    gstage[6, :, 64:128] = gacc[:, 192:256].astype(BF16)
+
+    wait_text(9, 10, 12, 13)
+    for block in (2, 3, 4):
+        send_text_grad(block)
 
     def owner(k):
         return lax.rem(chip + 1 + k, 8)
@@ -295,28 +301,35 @@
 
     def to_owner(k):
         return remote(rstage.at[k], rrecv.at[chip], rsend.at[k], rsem.at[chip], (me_dp, owner(k) * 2 + core))
+
+    def to_mate_part(k):
+        theirs = pl.ds(pl.multiple_of(owner(k) * 256 + (1 - core) * 128, 128), 128)
+        pstage[k] = gimg[theirs, :].astype(BF16)
+        from_mate(k).start()
 
     def chip_sum(k):
         mine = pl.ds(pl.multiple_of(owner(k) * 256 + core * 128, 128), 128)
         from_mate(k).wait_recv()
         return gimg[mine, :] + precv[k].astype(F32)
 
-    @pl.loop(0, 8)
-    def _(k):
-        r = owner(k)
-        chunk(3, r)
-        theirs = pl.ds(pl.multiple_of(r * 256 + (1 - core) * 128, 128), 128)
-        pstage[k] = gimg[theirs, :].astype(BF16)
-        from_mate(k).start()
-
-        @pl.when(k > 0)
-        def _():
-            rstage[k - 1] = chip_sum(k - 1).astype(BF16)
-            to_owner(k - 1).start()
-
-    stage_text_grads(3)
-    send_text_grad(3, 0, group(2, 0))
-    send_text_grad(3, 1, group(2, 1))
+    def pass_on(k):
+        rstage[k] = chip_sum(k).astype(BF16)
+        to_owner(k).start()
+
+    coef = coef_of(3, owner(0))
+    for k in range(8):
+        later = coef_of(3, owner(k + 1)) if k < 7 else None
+        grads_of(3, owner(k), coef, k == 0)
+        to_mate_part(k)
+        if k > 0:
+            pass_on(k - 1)
+        coef = later
+
+    gstage[6, :, 0:64] = gacc[:, 0:64].astype(BF16)
+    gstage[5, :, 64:128] = gacc[:, 64:128].astype(BF16)
+    gstage[7] = gacc[:, 128:256].astype(BF16)
+    for block in (5, 6, 7):
+        send_text_grad(block)
 
     rown[...] = chip_sum(7)
     for j in range(1, 8):
@@ -356,13 +369,9 @@
         sends.append(copy)
 
     text_sum = gown[...]
-    for pair in range(4):
-        for k in range(2):
-            if (pair, k) != (0, 0):
-                remote(
-                    gstage.at[pair, k], grecv.at[pair, k], gsend.at[0], gsem.at[pair * 2 + k], group(0, 1)
-                ).wait_recv()
-                text_sum = text_sum + grecv[pair, k].astype(F32)
+    for block in range(1, 8):
+        remote(gstage.at[block], grecv.at[block], gsend.at[block], gsem.at[block], across).wait_recv()
+        text_sum = text_sum + grecv[block].astype(F32)
     text_grad = text_sum.T
     unit, inverse = unit_of(rawtxt[...])
     gt_ref[...] = (text_grad - unit * jnp.sum(unit * text_grad, axis=1, keepdims=True)) * inverse
@@ -389,6 +398,12 @@
         @pl.when(k < 7)
         def _():
             to_owner(k).wait_send()
+
+
+def hand_over(*refs):
+    half = len(refs) // 2
+    for source, target in zip(refs[:half], refs[half:]):
+        target[...] = source[...]
 
 
 def per_device(images, head, tea_img, stu_txt, tea_txt):
@@ -414,12 +429,12 @@
             pltpu.VMEM((8, 2, 48, 768), BF16),
             pltpu.VMEM((2048, 768), BF16),
             pltpu.VMEM((8, 768, 256), BF16),
-            pltpu.VMEM((4, 2, 128, 2304), BF16),
+            pltpu.VMEM((4, 256, 2304), BF16),
             pltpu.VMEM((2048, 768), F32),
             pltpu.VMEM((768, 256), F32),
             pltpu.VMEM((768, 128), F32),
-            pltpu.VMEM((4, 2, 768, 128), BF16),
-            pltpu.VMEM((4, 2, 768, 128), BF16),
+            pltpu.VMEM((8, 768, 128), BF16),
+            pltpu.VMEM((8, 768, 128), BF16),
             pltpu.VMEM((8, 128, 768), BF16),
             pltpu.VMEM((8, 128, 768), BF16),
             pltpu.VMEM((8, 128, 768), BF16),
@@ -436,8 +451,8 @@
             dma((4,)),
             dma((8,)),
             dma((9,)),
-            dma((9,)),
-            dma((9,)),
+            dma((14,)),
+            dma((14,)),
             dma((8,)),
             dma((8,)),
             dma((8,)),
@@ -455,6 +470,13 @@
             collective_id=0, has_side_effects=True, vmem_limit_bytes=60 * 1024 * 1024
         ),
     )(images, head.T, tea_img, stu_txt, tea_txt)
+    grad_images, grad_head, grad_text = pl.pallas_call(
+        hand_over,
+        name="hand_over",
+        out_shape=tuple(jax.ShapeDtypeStruct(a.shape, a.dtype) for a in (grad_images, grad_head, grad_text)),
+        in_specs=[vmem_spec] * 3,
+        out_specs=(vmem_spec,) * 3,
+    )(grad_images, grad_head, grad_text)
     return (grad_images, grad_head.T, grad_text)
 
 

time: 110 us -> 100 us (0.909)
  local copies, waits for them, and re-layouts: 5.11 us -> 0 us
  Pallas kernels: 104 us -> 99.6 us
    pallas_call x1, Pallas kernels: 104 us -> 97.5 us  [per_device(): pl.pallas_call(functools.partial(kernel, factor), name='distill', out_sha...]
    unnamed x3 -> x0, local copies, waits for them, and re-layouts: 5.11 us -> none
    pallas_call x0 -> x1, Pallas kernels: none -> 2.13 us  [per_device(): pl.pallas_call(hand_over, name='hand_over', out_shape=tuple((jax.ShapeDty...]
where the time goes in v2:
time: 100 us
  Pallas kernels  99.6 us (100%)
    pallas_call x1, Pallas kernels, per_device(): pl.pallas_call(functools.partial(kernel, factor), name='distill', out_sha...  97.5 us
    pallas_call x1, Pallas kernels, per_device(): pl.pallas_call(hand_over, name='hand_over', out_shape=tuple((jax.ShapeDty...  2.13 us

profile of v2, /device:TPU:0, one launch (start us, length us, event | category | flops | bytes accessed | tf_op | source)
XLA Modules:
  0.0 100.2 jit_solution(2202419510553418924)
XLA Ops:
  0.6 97.5 %distill.1 = (f32[128,768]{1,0:T(8,128)}, f32[48,768]{1,0:T(8,128)}, f32[128,768]{1,0:T(8,128)}) custom-call(bf16[2048,768]{1,0:T(8,128)(2,1)} %images_hbm.1, bf16[48,768]{1,0:T(8,128)(2,1)} %bitcast.2, bf16[2048,1536]{1,0:T(8,128)(2,1)} %tea_hbm.1, bf16[128,768]{1,0:T(8,128)(2,1)} %txt_hbm.1, bf16[128,1536]{1,0:T(8,128)(2,1)} %teatxt_hbm.1), custom_call_target="tpu_custom_call" | custom-call | tf_op jit(solution)/shard_map/distill/pallas_call | solution.py:414
  98.1 2.1 %hand_over.1 = (f32[128,768]{1,0:T(8,128)}, f32[48,768]{1,0:T(8,128)}, f32[128,768]{1,0:T(8,128)}) custom-call(f32[128,768]{1,0:T(8,128)} %get-tuple-element.9.refs_0_, f32[48,768]{1,0:T(8,128)} %get-tuple-element.10.refs_1_, f32[128,768]{1,0:T(8,128)} %get-tuple-element.11.refs_2_), custom_call_target="tpu_custom_call" | custom-call | tf_op jit(solution)/shard_map/hand_over/pallas_call | solution.py:473

commit v3 on v2

--- a/solution.py
+++ b/solution.py
@@ -58,10 +58,13 @@
     rstage,
     rrecv,
     rown,
-    unit_own,
-    inv_own,
-    astage,
-    arecv,
+    units,
+    invs,
+    hacc,
+    hpstage,
+    hprecv,
+    hrstage,
+    hrrecv,
     xstage,
     xrecv,
     ystage,
@@ -77,8 +80,10 @@
     psem,
     rsend,
     rsem,
-    asend,
-    asem,
+    hpsend,
+    hpsem,
+    hrsend,
+    hrsem,
     xsend,
     xsem,
     ysend,
@@ -123,7 +128,7 @@
         load.start()
 
     partners = [group(dx, side) for dx in range(4) for side in range(2) if (dx, side) != (0, 0)]
-    partners += [(me_dp, lax.rem(me_t + j, 16)) for j in range(1, 16)]
+    partners += [plane(j) for j in range(1, 8)] + [(me_dp, mate)]
     partners += [((1 - y_hi) * 4 + x, me_t)]
     barrier = pltpu.get_barrier_semaphore()
     for device in partners:
@@ -200,7 +205,9 @@
     def project(r):
         rows = pl.ds(pl.multiple_of(r * 256, 256), 256)
         proj = dot(images[rows, :], head_all(), NT).astype(BF16)
-        unit = unit_of(proj)[0]
+        unit, inverse = unit_of(proj)
+        units[rows, :] = unit
+        invs[rows, :] = inverse
         img[rows, :] = unit.astype(BF16)
         img_t[r] = unit.T.astype(BF16)
 
@@ -215,11 +222,6 @@
     @pl.loop(4, 8)
     def _(r):
         project(r)
-
-    own_rows = pl.ds(pl.multiple_of(me_t * 128, 128), 128)
-    unit, inverse = unit_of(dot(images[own_rows, :], head_all(), NT).astype(BF16))
-    unit_own[...] = unit
-    inv_own[...] = inverse
 
     def coef_of(step, r):
         rows = pl.ds(pl.multiple_of(r * 256, 256), 256)
@@ -289,9 +291,9 @@
     gstage[5, :, 0:64] = gacc[:, 128:192].astype(BF16)
     gstage[6, :, 64:128] = gacc[:, 192:256].astype(BF16)
 
-    wait_text(9, 10, 12, 13)
     for block in (2, 3, 4):
         send_text_grad(block)
+    wait_text(9, 10, 12, 13)
 
     def owner(k):
         return lax.rem(chip + 1 + k, 8)
@@ -316,14 +318,32 @@
         rstage[k] = chip_sum(k).astype(BF16)
         to_owner(k).start()
 
+    def head_part(r, first):
+        rows = pl.ds(pl.multiple_of(r * 256, 256), 256)
+        grad, unit = gimg[rows, :], units[rows, :]
+        row_dot = jnp.sum(unit * grad, axis=1, keepdims=True)
+        grad_proj = (grad - unit * row_dot) * invs[rows, :]
+        part = dot(grad_proj.T.astype(BF16), images[rows, :]).reshape(8, 2, 48, 768)
+        if first:
+            hacc[...] = part
+        else:
+            hacc[...] += part
+
+    early = 3
     coef = coef_of(3, owner(0))
     for k in range(8):
         later = coef_of(3, owner(k + 1)) if k < 7 else None
         grads_of(3, owner(k), coef, k == 0)
         to_mate_part(k)
-        if k > 0:
+        head_part(owner(k), k == 0)
+        if 0 < k <= early:
             pass_on(k - 1)
         coef = later
+
+    hpstage[...] = hacc[:, 1 - core].astype(BF16)
+    head_swap = remote(hpstage, hprecv, hpsend.at[0], hpsem.at[0], (me_dp, mate))
+    head_swap.start()
+    sends.append(head_swap)
 
     gstage[6, :, 0:64] = gacc[:, 0:64].astype(BF16)
     gstage[5, :, 64:128] = gacc[:, 64:128].astype(BF16)
@@ -331,37 +351,24 @@
     for block in (5, 6, 7):
         send_text_grad(block)
 
-    rown[...] = chip_sum(7)
+    head_swap.wait_recv()
+    hrstage[...] = (hacc[:, core] + hprecv[...].astype(F32)).astype(BF16)
     for j in range(1, 8):
         other = lax.rem(chip + j, 8)
-        remote(rstage.at[0], rrecv.at[other], rsend.at[0], rsem.at[other], plane(j)).wait_recv()
-        rown[...] += rrecv[other].astype(F32)
-
-    total = rown[...]
-    unit = unit_own[...]
-    row_dot = jnp.sum(unit * total, axis=1, keepdims=True)
-    grad_proj = (total - unit * row_dot) * inv_own[...]
-    astage[...] = grad_proj.T.astype(BF16).reshape(16, 48, 128)
-    arecv[me_t] = astage[me_t]
-    scatter = []
-    for j in range(1, 16):
-        other = lax.rem(me_t + j, 16)
-        copy = remote(astage.at[other], arecv.at[me_t], asend.at[j - 1], asem.at[me_t], (me_dp, other))
+        copy = remote(hrstage.at[other], hrrecv.at[chip], hrsend.at[j - 1], hrsem.at[chip], plane(j))
         copy.start()
-        scatter.append(copy)
-    sends += scatter
-
-    gi_ref[...] = dot(grad_proj.astype(BF16), head_all())
-
-    for j in range(1, 16):
-        other = lax.rem(me_t + j, 16)
-        remote(astage.at[other], arecv.at[other], asend.at[j - 1], asem.at[other], (me_dp, other)).wait_recv()
-
-    head_part = jnp.zeros((48, 768), F32)
-    for s in range(8):
-        pieces = jnp.concatenate([arecv[2 * s], arecv[2 * s + 1]], axis=1)
-        head_part += dot(pieces, images[s * 256 : (s + 1) * 256, :])
-    xstage[...] = head_part.astype(BF16)
+        sends.append(copy)
+
+    for k in range(early, 7):
+        pass_on(k)
+    rown[...] = chip_sum(7)
+
+    head_sum = hrstage[chip].astype(F32)
+    for j in range(1, 8):
+        other = lax.rem(chip + j, 8)
+        remote(hrstage.at[0], hrrecv.at[other], hrsend.at[0], hrsem.at[other], plane(j)).wait_recv()
+        head_sum = head_sum + hrrecv[other].astype(F32)
+    xstage[...] = head_sum.astype(BF16)
     xrecv[x] = xstage[...]
     for j in range(1, 4):
         copy = remote(xstage, xrecv.at[x], xsend.at[j - 1], xsem.at[x], (at_x(j), me_t))
@@ -384,8 +391,19 @@
     ).astype(BF16)
     swap = remote(ystage, yrecv, ysend.at[0], ysem.at[0], ((1 - y_hi) * 4 + x, me_t))
     swap.start()
+    sends.append(swap)
+
+    for j in range(1, 8):
+        other = lax.rem(chip + j, 8)
+        remote(rstage.at[0], rrecv.at[other], rsend.at[0], rsem.at[other], plane(j)).wait_recv()
+        rown[...] += rrecv[other].astype(F32)
+    own_rows = pl.ds(pl.multiple_of(me_t * 128, 128), 128)
+    total, unit = rown[...], units[own_rows, :]
+    row_dot = jnp.sum(unit * total, axis=1, keepdims=True)
+    grad_proj = (total - unit * row_dot) * invs[own_rows, :]
+    gi_ref[...] = dot(grad_proj.astype(BF16), head_all())
+
     swap.wait_recv()
-    sends.append(swap)
     gh_ref[...] = ystage[...].astype(F32) + yrecv[...].astype(F32)
 
     for copy in sends:
@@ -440,10 +458,13 @@
             pltpu.VMEM((8, 128, 768), BF16),
             pltpu.VMEM((8, 128, 768), BF16),
             pltpu.VMEM((128, 768), F32),
-            pltpu.VMEM((128, 768), F32),
-            pltpu.VMEM((128, 1), F32),
-            pltpu.VMEM((16, 48, 128), BF16),
-            pltpu.VMEM((16, 48, 128), BF16),
+            pltpu.VMEM((2048, 768), F32),
+            pltpu.VMEM((2048, 1), F32),
+            pltpu.VMEM((8, 2, 48, 768), F32),
+            pltpu.VMEM((8, 48, 768), BF16),
+            pltpu.VMEM((8, 48, 768), BF16),
+            pltpu.VMEM((8, 48, 768), BF16),
+            pltpu.VMEM((8, 48, 768), BF16),
             pltpu.VMEM((48, 768), BF16),
             pltpu.VMEM((4, 48, 768), BF16),
             pltpu.VMEM((48, 768), BF16),
@@ -459,8 +480,10 @@
             dma((8,)),
             dma((8,)),
             dma((8,)),
-            dma((15,)),
-            dma((16,)),
+            dma((1,)),
+            dma((1,)),
+            dma((7,)),
+            dma((8,)),
             dma((3,)),
             dma((4,)),
             dma((1,)),

time: 100 us -> 94.8 us (0.948); the launches traced: 100 us -> 93.9 us
  Pallas kernels: 99.6 us -> 93.2 us
    pallas_call x1, Pallas kernels: 97.5 us -> 91.1 us  [per_device(): pl.pallas_call(functools.partial(kernel, factor), name='distill', out_sha...]
where the time goes in v3:
time: 94.8 us; the launch traced here: 93.9 us
  Pallas kernels  93.2 us (98%)
    pallas_call x1, Pallas kernels, per_device(): pl.pallas_call(functools.partial(kernel, factor), name='distill', out_sha...  91.1 us
    pallas_call x1, Pallas kernels, per_device(): pl.pallas_call(hand_over, name='hand_over', out_shape=tuple((jax.ShapeDty...  2.13 us

profile of v3, /device:TPU:0, one launch (start us, length us, event | category | flops | bytes accessed | tf_op | source)
XLA Modules:
  0.0 93.9 jit_solution(10137471174734949763)
XLA Ops:
  0.6 91.1 %distill.1 = (f32[128,768]{1,0:T(8,128)}, f32[48,768]{1,0:T(8,128)}, f32[128,768]{1,0:T(8,128)}) custom-call(bf16[2048,768]{1,0:T(8,128)(2,1)} %images_hbm.1, bf16[48,768]{1,0:T(8,128)(2,1)} %bitcast.2, bf16[2048,1536]{1,0:T(8,128)(2,1)} %tea_hbm.1, bf16[128,768]{1,0:T(8,128)(2,1)} %txt_hbm.1, bf16[128,1536]{1,0:T(8,128)(2,1)} %teatxt_hbm.1), custom_call_target="tpu_custom_call" | custom-call | tf_op jit(solution)/shard_map/distill/pallas_call | solution.py:432
  91.7 2.1 %hand_over.1 = (f32[128,768]{1,0:T(8,128)}, f32[48,768]{1,0:T(8,128)}, f32[128,768]{1,0:T(8,128)}) custom-call(f32[128,768]{1,0:T(8,128)} %get-tuple-element.9.refs_0_, f32[48,768]{1,0:T(8,128)} %get-tuple-element.10.refs_1_, f32[128,768]{1,0:T(8,128)} %get-tuple-element.11.refs_2_), custom_call_target="tpu_custom_call" | custom-call | tf_op jit(solution)/shard_map/hand_over/pallas_call | solution.py:496

commit v4 on v3

--- a/solution.py
+++ b/solution.py
@@ -67,8 +67,6 @@
     hrrecv,
     xstage,
     xrecv,
-    ystage,
-    yrecv,
     lsem,
     hsend,
     hrecv,
@@ -86,8 +84,6 @@
     hrsem,
     xsend,
     xsem,
-    ysend,
-    ysem,
 ):
     me_dp = lax.axis_index("dp")
     me_t = lax.axis_index("tensor")
@@ -129,7 +125,7 @@
 
     partners = [group(dx, side) for dx in range(4) for side in range(2) if (dx, side) != (0, 0)]
     partners += [plane(j) for j in range(1, 8)] + [(me_dp, mate)]
-    partners += [((1 - y_hi) * 4 + x, me_t)]
+    partners += [(across_x(dx), me_t) for dx in range(4)]
     barrier = pltpu.get_barrier_semaphore()
     for device in partners:
         pl.semaphore_signal(barrier, inc=1, device_id=device, device_id_type=MESH)
@@ -150,7 +146,7 @@
         (1, 128), (1, 192),
         (2, 0), (2, 64),
         (2, 128), (3, 64),
-        (3, 0), (2, 192),
+        (2, 192), (3, 0),
         (3, 128), (3, 192),
     ]
 
@@ -218,6 +214,9 @@
     wait_text(4, 3)
     send_text(places[4], 6, 6, ahead)
     send_text(places[3], 7, 7, behind)
+    wait_text(0)
+    send_text(places[0], 8, 8, ahead)
+    send_text(places[0], 10, 11, behind)
 
     @pl.loop(4, 8)
     def _(r):
@@ -246,9 +245,11 @@
         else:
             gacc[...] += text_part
 
-    def run_step(step):
+    def run_step(step, pause=None, meanwhile=None):
         coef = coef_of(step, 0)
         for r in range(8):
+            if r == pause:
+                meanwhile()
             later = coef_of(step, r + 1) if r < 7 else None
             grads_of(step, r, coef, r == 0)
             coef = later
@@ -267,33 +268,34 @@
         copy.start()
         sends.append(copy)
 
-    wait_text(0, 1)
-    send_text(places[0], 8, 8, ahead)
+    wait_text(1)
+    send_text(places[1], 9, 10, ahead)
     send_text(places[1], 11, 9, behind)
-    send_text(places[1], 9, 10, ahead)
-    send_text(places[0], 10, 11, behind)
     run_step(0)
     gown[...] = gacc[:, 0:128]
     gstage[1] = gacc[:, 128:256].astype(BF16)
     send_text_grad(1)
 
     wait_text(2, 5)
-    run_step(1)
+
+    def second_across():
+        wait_text(6, 7)
+        send_text(places[6], 12, 12, across)
+        send_text(places[7], 13, 13, across)
+
+    run_step(1, 5, second_across)
     gstage[2] = gacc[:, 0:128].astype(BF16)
     gstage[3] = gacc[:, 128:256].astype(BF16)
 
-    wait_text(6, 7)
-    send_text(places[6], 12, 12, across)
-    send_text(places[7], 13, 13, across)
-    wait_text(8, 11)
+    wait_text(8, 10)
     run_step(2)
     gstage[4] = gacc[:, 0:128].astype(BF16)
     gstage[5, :, 0:64] = gacc[:, 128:192].astype(BF16)
-    gstage[6, :, 64:128] = gacc[:, 192:256].astype(BF16)
+    gstage[6, :, 0:64] = gacc[:, 192:256].astype(BF16)
 
     for block in (2, 3, 4):
         send_text_grad(block)
-    wait_text(9, 10, 12, 13)
+    wait_text(9, 11, 12, 13)
 
     def owner(k):
         return lax.rem(chip + 1 + k, 8)
@@ -329,15 +331,15 @@
         else:
             hacc[...] += part
 
-    early = 3
+    lag, early = 4, 4
     coef = coef_of(3, owner(0))
     for k in range(8):
         later = coef_of(3, owner(k + 1)) if k < 7 else None
         grads_of(3, owner(k), coef, k == 0)
         to_mate_part(k)
         head_part(owner(k), k == 0)
-        if 0 < k <= early:
-            pass_on(k - 1)
+        if k >= lag:
+            pass_on(k - lag)
         coef = later
 
     hpstage[...] = hacc[:, 1 - core].astype(BF16)
@@ -345,7 +347,7 @@
     head_swap.start()
     sends.append(head_swap)
 
-    gstage[6, :, 0:64] = gacc[:, 0:64].astype(BF16)
+    gstage[6, :, 64:128] = gacc[:, 0:64].astype(BF16)
     gstage[5, :, 64:128] = gacc[:, 64:128].astype(BF16)
     gstage[7] = gacc[:, 128:256].astype(BF16)
     for block in (5, 6, 7):
@@ -369,9 +371,10 @@
         remote(hrstage.at[0], hrrecv.at[other], hrsend.at[0], hrsem.at[other], plane(j)).wait_recv()
         head_sum = head_sum + hrrecv[other].astype(F32)
     xstage[...] = head_sum.astype(BF16)
-    xrecv[x] = xstage[...]
-    for j in range(1, 4):
-        copy = remote(xstage, xrecv.at[x], xsend.at[j - 1], xsem.at[x], (at_x(j), me_t))
+    xrecv[me_dp] = xstage[...]
+    others = [at_x(1), at_x(3), across_x(0), at_x(2), across_x(1), across_x(3), across_x(2)]
+    for j, other in enumerate(others):
+        copy = remote(xstage, xrecv.at[me_dp], xsend.at[j], xsem.at[me_dp], (other, me_t))
         copy.start()
         sends.append(copy)
 
@@ -382,16 +385,6 @@
     text_grad = text_sum.T
     unit, inverse = unit_of(rawtxt[...])
     gt_ref[...] = (text_grad - unit * jnp.sum(unit * text_grad, axis=1, keepdims=True)) * inverse
-
-    for j in range(1, 4):
-        other = lax.rem(x + j, 4)
-        remote(xstage, xrecv.at[other], xsend.at[j - 1], xsem.at[other], (at_x(j), me_t)).wait_recv()
-    ystage[...] = (
-        (xrecv[0].astype(F32) + xrecv[1].astype(F32)) + (xrecv[2].astype(F32) + xrecv[3].astype(F32))
-    ).astype(BF16)
-    swap = remote(ystage, yrecv, ysend.at[0], ysem.at[0], ((1 - y_hi) * 4 + x, me_t))
-    swap.start()
-    sends.append(swap)
 
     for j in range(1, 8):
         other = lax.rem(chip + j, 8)
@@ -403,8 +396,12 @@
     grad_proj = (total - unit * row_dot) * invs[own_rows, :]
     gi_ref[...] = dot(grad_proj.astype(BF16), head_all())
 
-    swap.wait_recv()
-    gh_ref[...] = ystage[...].astype(F32) + yrecv[...].astype(F32)
+    for other in others:
+        remote(xstage, xrecv.at[other], xsend.at[0], xsem.at[other], (other, me_t)).wait_recv()
+    head_grad = xrecv[0].astype(F32)
+    for d in range(1, 8):
+        head_grad = head_grad + xrecv[d].astype(F32)
+    gh_ref[...] = head_grad
 
     for copy in sends:
         copy.wait_send()
@@ -466,9 +463,7 @@
             pltpu.VMEM((8, 48, 768), BF16),
             pltpu.VMEM((8, 48, 768), BF16),
             pltpu.VMEM((48, 768), BF16),
-            pltpu.VMEM((4, 48, 768), BF16),
-            pltpu.VMEM((48, 768), BF16),
-            pltpu.VMEM((48, 768), BF16),
+            pltpu.VMEM((8, 48, 768), BF16),
             dma((4,)),
             dma((8,)),
             dma((9,)),
@@ -484,10 +479,8 @@
             dma((1,)),
             dma((7,)),
             dma((8,)),
-            dma((3,)),
-            dma((4,)),
-            dma((1,)),
-            dma((1,)),
+            dma((7,)),
+            dma((8,)),
         ],
         compiler_params=pltpu.CompilerParams(
             collective_id=0, has_side_effects=True, vmem_limit_bytes=60 * 1024 * 1024

time: 94.8 us -> 99.4 us (1.049)
  Pallas kernels: 93.2 us -> 97.5 us
    pallas_call x1, Pallas kernels: 91.1 us -> 95.4 us  [per_device(): pl.pallas_call(functools.partial(kernel, factor), name='distill', out_sha...]
where the time goes in v4:
time: 99.4 us; the launch traced here: 98.2 us
  Pallas kernels  97.5 us (98%)
    pallas_call x1, Pallas kernels, per_device(): pl.pallas_call(functools.partial(kernel, factor), name='distill', out_sha...  95.4 us
    pallas_call x1, Pallas kernels, per_device(): pl.pallas_call(hand_over, name='hand_over', out_shape=tuple((jax.ShapeDty...  2.13 us

profile of v4, /device:TPU:0, one launch (start us, length us, event | category | flops | bytes accessed | tf_op | source)
XLA Modules:
  0.0 98.2 jit_solution(2337891251113375817)
XLA Ops:
  0.6 95.4 %distill.1 = (f32[128,768]{1,0:T(8,128)}, f32[48,768]{1,0:T(8,128)}, f32[128,768]{1,0:T(8,128)}) custom-call(bf16[2048,768]{1,0:T(8,128)(2,1)} %images_hbm.1, bf16[48,768]{1,0:T(8,128)(2,1)} %bitcast.2, bf16[2048,1536]{1,0:T(8,128)(2,1)} %tea_hbm.1, bf16[128,768]{1,0:T(8,128)(2,1)} %txt_hbm.1, bf16[128,1536]{1,0:T(8,128)(2,1)} %teatxt_hbm.1), custom_call_target="tpu_custom_call" | custom-call | tf_op jit(solution)/shard_map/distill/pallas_call | solution.py:429
  96.0 2.1 %hand_over.1 = (f32[128,768]{1,0:T(8,128)}, f32[48,768]{1,0:T(8,128)}, f32[128,768]{1,0:T(8,128)}) custom-call(f32[128,768]{1,0:T(8,128)} %get-tuple-element.9.refs_0_, f32[48,768]{1,0:T(8,128)} %get-tuple-element.10.refs_1_, f32[128,768]{1,0:T(8,128)} %get-tuple-element.11.refs_2_), custom_call_target="tpu_custom_call" | custom-call | tf_op jit(solution)/shard_map/hand_over/pallas_call | solution.py:489

commit v5 on v3

--- a/solution.py
+++ b/solution.py
@@ -96,6 +96,7 @@
     chip = me_t // 2
     core = me_t % 2
     y_lo = me_t // 8
+    z = chip % 4
     flip_t = (1 - y_lo) * 8 + me_t % 8
     mate = chip * 2 + (1 - core)
 
@@ -150,7 +151,7 @@
         (1, 128), (1, 192),
         (2, 0), (2, 64),
         (2, 128), (3, 64),
-        (3, 0), (2, 192),
+        (2, 192), (3, 0),
         (3, 128), (3, 192),
     ]
 
@@ -218,6 +219,9 @@
     wait_text(4, 3)
     send_text(places[4], 6, 6, ahead)
     send_text(places[3], 7, 7, behind)
+    wait_text(0)
+    send_text(places[0], 8, 8, ahead)
+    send_text(places[0], 10, 11, behind)
 
     @pl.loop(4, 8)
     def _(r):
@@ -246,9 +250,11 @@
         else:
             gacc[...] += text_part
 
-    def run_step(step):
+    def run_step(step, pause=None, meanwhile=None):
         coef = coef_of(step, 0)
         for r in range(8):
+            if r == pause:
+                meanwhile()
             later = coef_of(step, r + 1) if r < 7 else None
             grads_of(step, r, coef, r == 0)
             coef = later
@@ -267,36 +273,40 @@
         copy.start()
         sends.append(copy)
 
-    wait_text(0, 1)
-    send_text(places[0], 8, 8, ahead)
+    wait_text(1)
+    send_text(places[1], 9, 10, ahead)
     send_text(places[1], 11, 9, behind)
-    send_text(places[1], 9, 10, ahead)
-    send_text(places[0], 10, 11, behind)
     run_step(0)
     gown[...] = gacc[:, 0:128]
     gstage[1] = gacc[:, 128:256].astype(BF16)
-    send_text_grad(1)
 
     wait_text(2, 5)
-    run_step(1)
+
+    def second_across():
+        wait_text(6, 7)
+        send_text(places[6], 12, 12, across)
+        send_text(places[7], 13, 13, across)
+        send_text_grad(1)
+
+    run_step(1, 5, second_across)
     gstage[2] = gacc[:, 0:128].astype(BF16)
     gstage[3] = gacc[:, 128:256].astype(BF16)
 
-    wait_text(6, 7)
-    send_text(places[6], 12, 12, across)
-    send_text(places[7], 13, 13, across)
-    wait_text(8, 11)
+    wait_text(8, 10)
     run_step(2)
     gstage[4] = gacc[:, 0:128].astype(BF16)
     gstage[5, :, 0:64] = gacc[:, 128:192].astype(BF16)
-    gstage[6, :, 64:128] = gacc[:, 192:256].astype(BF16)
+    gstage[6, :, 0:64] = gacc[:, 192:256].astype(BF16)
 
     for block in (2, 3, 4):
         send_text_grad(block)
-    wait_text(9, 10, 12, 13)
+    wait_text(9, 11, 12, 13)
+
+    route = [(1, 1), (0, 3), (1, 3), (0, 1), (1, 0), (1, 2), (0, 2), (0, 0)]
 
     def owner(k):
-        return lax.rem(chip + 1 + k, 8)
+        dy, dz = route[k]
+        return lax.rem(y_lo + dy, 2) * 4 + lax.rem(z + dz, 4)
 
     def from_mate(k):
         return remote(pstage.at[k], precv.at[k], psend.at[k], psem.at[k], (me_dp, mate))
@@ -314,38 +324,48 @@
         from_mate(k).wait_recv()
         return gimg[mine, :] + precv[k].astype(F32)
 
-    def pass_on(k):
-        rstage[k] = chip_sum(k).astype(BF16)
-        to_owner(k).start()
-
-    def head_part(r, first):
-        rows = pl.ds(pl.multiple_of(r * 256, 256), 256)
-        grad, unit = gimg[rows, :], units[rows, :]
-        row_dot = jnp.sum(unit * grad, axis=1, keepdims=True)
-        grad_proj = (grad - unit * row_dot) * invs[rows, :]
-        part = dot(grad_proj.T.astype(BF16), images[rows, :]).reshape(8, 2, 48, 768)
-        if first:
-            hacc[...] = part
+    lag, early = 3, 3
+    pieces = {}
+
+    def take(k):
+        mine = pl.ds(pl.multiple_of(owner(k) * 256 + core * 128, 128), 128)
+        total = chip_sum(k)
+        if k < 7:
+            rstage[k] = total.astype(BF16)
         else:
-            hacc[...] += part
-
-    early = 3
+            rown[...] = total
+        if k < early:
+            to_owner(k).start()
+        unit = units[mine, :]
+        row_dot = jnp.sum(unit * total, axis=1, keepdims=True)
+        grad_proj = (total - unit * row_dot) * invs[mine, :]
+        pieces[k] = (grad_proj.T.astype(BF16), images[mine, :])
+        if k % 2:
+            left = jnp.concatenate([pieces[k - 1][0], pieces[k][0]], axis=1)
+            right = jnp.concatenate([pieces[k - 1][1], pieces[k][1]], axis=0)
+            part = dot(left, right).reshape(8, 2, 48, 768)
+            if k == 1:
+                hacc[...] = part
+            else:
+                hacc[...] += part
+
     coef = coef_of(3, owner(0))
     for k in range(8):
         later = coef_of(3, owner(k + 1)) if k < 7 else None
         grads_of(3, owner(k), coef, k == 0)
         to_mate_part(k)
-        head_part(owner(k), k == 0)
-        if 0 < k <= early:
-            pass_on(k - 1)
+        if k >= lag:
+            take(k - lag)
         coef = later
+    for k in range(8 - lag, 8):
+        take(k)
 
     hpstage[...] = hacc[:, 1 - core].astype(BF16)
     head_swap = remote(hpstage, hprecv, hpsend.at[0], hpsem.at[0], (me_dp, mate))
     head_swap.start()
     sends.append(head_swap)
 
-    gstage[6, :, 0:64] = gacc[:, 0:64].astype(BF16)
+    gstage[6, :, 64:128] = gacc[:, 0:64].astype(BF16)
     gstage[5, :, 64:128] = gacc[:, 64:128].astype(BF16)
     gstage[7] = gacc[:, 128:256].astype(BF16)
     for block in (5, 6, 7):
@@ -360,8 +380,7 @@
         sends.append(copy)
 
     for k in range(early, 7):
-        pass_on(k)
-    rown[...] = chip_sum(7)
+        to_owner(k).start()
 
     head_sum = hrstage[chip].astype(F32)
     for j in range(1, 8):
@@ -409,12 +428,9 @@
     for copy in sends:
         copy.wait_send()
 
-    @pl.loop(0, 8)
-    def _(k):
+    for k in range(8):
         from_mate(k).wait_send()
-
-        @pl.when(k < 7)
-        def _():
+        if k < 7:
             to_owner(k).wait_send()
 
 

time: 94.8 us -> 89.9 us (0.948)
  the two profiles are of different devices: /device:TPU:0 before, /device:TPU:44 now
where the time goes in v5:
time: 89.9 us; the launch traced here: 89.8 us
  Pallas kernels  89.1 us (99%)
    pallas_call x1, Pallas kernels, per_device(): pl.pallas_call(functools.partial(kernel, factor), name='distill', out_sha...  87 us
    pallas_call x1, Pallas kernels, per_device(): pl.pallas_call(hand_over, name='hand_over', out_shape=tuple((jax.ShapeDty...  2.13 us

profile of v5, /device:TPU:44, one launch (start us, length us, event | category | flops | bytes accessed | tf_op | source)
XLA Modules:
  0.0 89.8 jit_solution(14069167192269288005)
XLA Ops:
  0.6 87.0 %distill.1 = (f32[128,768]{1,0:T(8,128)}, f32[48,768]{1,0:T(8,128)}, f32[128,768]{1,0:T(8,128)}) custom-call(bf16[2048,768]{1,0:T(8,128)(2,1)} %images_hbm.1, bf16[48,768]{1,0:T(8,128)(2,1)} %bitcast.2, bf16[2048,1536]{1,0:T(8,128)(2,1)} %tea_hbm.1, bf16[128,768]{1,0:T(8,128)(2,1)} %txt_hbm.1, bf16[128,1536]{1,0:T(8,128)(2,1)} %teatxt_hbm.1), custom_call_target="tpu_custom_call" | custom-call | tf_op jit(solution)/shard_map/distill/pallas_call | solution.py:448
  87.6 2.1 %hand_over.1 = (f32[128,768]{1,0:T(8,128)}, f32[48,768]{1,0:T(8,128)}, f32[128,768]{1,0:T(8,128)}) custom-call(f32[128,768]{1,0:T(8,128)} %get-tuple-element.9.refs_0_, f32[48,768]{1,0:T(8,128)} %get-tuple-element.10.refs_1_, f32[128,768]{1,0:T(8,128)} %get-tuple-element.11.refs_2_), custom_call_target="tpu_custom_call" | custom-call | tf_op jit(solution)/shard_map/hand_over/pallas_call | solution.py:512

commit v6 on v5

--- a/solution.py
+++ b/solution.py
@@ -288,7 +288,7 @@
         send_text(places[7], 13, 13, across)
         send_text_grad(1)
 
-    run_step(1, 5, second_across)
+    run_step(1, 2, second_across)
     gstage[2] = gacc[:, 0:128].astype(BF16)
     gstage[3] = gacc[:, 128:256].astype(BF16)
 
@@ -324,7 +324,7 @@
         from_mate(k).wait_recv()
         return gimg[mine, :] + precv[k].astype(F32)
 
-    lag, early = 3, 3
+    lag, early = 2, 3
     pieces = {}
 
     def take(k):
@@ -339,12 +339,12 @@
         unit = units[mine, :]
         row_dot = jnp.sum(unit * total, axis=1, keepdims=True)
         grad_proj = (total - unit * row_dot) * invs[mine, :]
-        pieces[k] = (grad_proj.T.astype(BF16), images[mine, :])
-        if k % 2:
-            left = jnp.concatenate([pieces[k - 1][0], pieces[k][0]], axis=1)
-            right = jnp.concatenate([pieces[k - 1][1], pieces[k][1]], axis=0)
+        pieces[k] = (grad_proj.astype(BF16).T, images[mine, :])
+        if k % 4 == 3:
+            left = jnp.concatenate([pieces[n][0] for n in range(k - 3, k + 1)], axis=1)
+            right = jnp.concatenate([pieces[n][1] for n in range(k - 3, k + 1)], axis=0)
             part = dot(left, right).reshape(8, 2, 48, 768)
-            if k == 1:
+            if k == 3:
                 hacc[...] = part
             else:
                 hacc[...] += part

time: 89.9 us -> 86 us (0.957)
  the two profiles are of different devices: /device:TPU:44 before, /device:TPU:0 now
where the time goes in v6:
time: 86 us; the launch traced here: 84.8 us
  Pallas kernels  84.2 us (98%)
    pallas_call x1, Pallas kernels, per_device(): pl.pallas_call(functools.partial(kernel, factor), name='distill', out_sha...  82 us
    pallas_call x1, Pallas kernels, per_device(): pl.pallas_call(hand_over, name='hand_over', out_shape=tuple((jax.ShapeDty...  2.13 us

profile of v6, /device:TPU:0, one launch (start us, length us, event | category | flops | bytes accessed | tf_op | source)
XLA Modules:
  0.0 84.8 jit_solution(15306267249940464865)
XLA Ops:
  0.6 82.0 %distill.1 = (f32[128,768]{1,0:T(8,128)}, f32[48,768]{1,0:T(8,128)}, f32[128,768]{1,0:T(8,128)}) custom-call(bf16[2048,768]{1,0:T(8,128)(2,1)} %images_hbm.1, bf16[48,768]{1,0:T(8,128)(2,1)} %bitcast.2, bf16[2048,1536]{1,0:T(8,128)(2,1)} %tea_hbm.1, bf16[128,768]{1,0:T(8,128)(2,1)} %txt_hbm.1, bf16[128,1536]{1,0:T(8,128)(2,1)} %teatxt_hbm.1), custom_call_target="tpu_custom_call" | custom-call | tf_op jit(solution)/shard_map/distill/pallas_call | solution.py:448
  82.7 2.1 %hand_over.1 = (f32[128,768]{1,0:T(8,128)}, f32[48,768]{1,0:T(8,128)}, f32[128,768]{1,0:T(8,128)}) custom-call(f32[128,768]{1,0:T(8,128)} %get-tuple-element.9.refs_0_, f32[48,768]{1,0:T(8,128)} %get-tuple-element.10.refs_1_, f32[128,768]{1,0:T(8,128)} %get-tuple-element.11.refs_2_), custom_call_target="tpu_custom_call" | custom-call | tf_op jit(solution)/shard_map/hand_over/pallas_call | solution.py:512
